TPU v7x, 512 devices: a whole 4x4x16 slice. The times are simulated.
512 devices in a mesh: seq: 64 (over z, y), head: 8 (over x, core).
Axes of the slice: x: 4, y: 4, z: 16, core: 2. Of those that a mesh axis runs over, the one named last changes fastest.
Arguments:
- queries: bfloat16 [16384, 4096], P('seq', 'head'), may hold values from -0.29882812 to 0.29882812
- keys: bfloat16 [16384, 4096], P('seq', 'head'), may hold values from -0.29882812 to 0.29882812
- values: bfloat16 [16384, 4096], P('seq', 'head'), may hold values from -0.59765625 to 0.59765625
- out_grad: bfloat16 [16384, 4096], P('seq', 'head'), may hold values from -6 to 6
- doc_lengths: int32 [32], replicated, may hold values from 1 to 1024, 16384 in all
Outputs:
- query_grad: bfloat16 [16384, 4096], P(('seq', 'head'))
- key_grad: bfloat16 [16384, 4096], P(('seq', 'head'))
- value_grad: bfloat16 [16384, 4096], P(('seq', 'head'))
Inputs may be any that keep to these rules, and one draw needn't show every extreme that they name: `doc_lengths`: the lengths sum to 16384 and the largest equals 1024.
All inputs are finite; a program needn't handle non-finite values.
Results may differ from a plain program's by a relative error of at most 0.0033.
Values may be sent and summed in bfloat16 or wider, within the bound.
A program may use at most 128 MiB of HBM per device.

v0:
```python
import jax
import jax.numpy as jnp
from jax import lax
from jax.sharding import PartitionSpec as P

HEAD_DIM = 128


def prefix(part, axis, combine, identity, reverse):
    count = lax.axis_size(axis)
    place = lax.axis_index(axis)
    ahead = count - 1 - place if reverse else place
    gathered = jax.tree.map(lambda a: lax.all_gather(a, axis), part)
    state = jax.tree.map(lambda a, e: jnp.zeros_like(a) + jnp.asarray(e, a.dtype), part, identity)

    def one(lap, state):
        source = count - 1 - lap if reverse else lap
        return combine(
            state, jax.tree.map(lambda a: lax.dynamic_index_in_dim(a, source, 0, False), gathered)
        )

    return lax.fori_loop(0, ahead, one, state)


def combine_pair(earlier, current):
    return (current[0] + (1.0 - current[1]) * earlier[0], jnp.maximum(earlier[1], current[1]))


def shards(queries, keys, values, out_grad, doc_lengths):
    rows_dev = queries.shape[0]
    width = queries.shape[1]
    head_count = width // HEAD_DIM
    shard_begin = lax.axis_index("seq") * rows_dev
    starts = jnp.cumsum(doc_lengths) - doc_lengths
    order = jnp.arange(rows_dev, dtype=jnp.int32)
    position = shard_begin + order
    before = starts[None, :] <= position[:, None]
    doc_index = jnp.sum(before.astype(jnp.int32), axis=1) - 1
    doc_begin = jnp.max(jnp.where(before, starts[None, :], 0), axis=1)
    first_rows = doc_begin < shard_begin
    last_rows = doc_index == doc_index[rows_dev - 1]
    has_start = jnp.any(doc_begin >= shard_begin).astype(jnp.float32)
    query_heads = queries.reshape(rows_dev, head_count, HEAD_DIM)
    key_heads = keys.reshape(rows_dev, head_count, HEAD_DIM)
    value_heads = values.reshape(rows_dev, head_count, HEAD_DIM)
    grad_heads = out_grad.reshape(rows_dev, head_count, HEAD_DIM)
    tail_keys = jnp.where(last_rows[:, None, None], key_heads, jnp.zeros_like(key_heads))
    tail_state = jnp.einsum(
        "lhd,lhe->hde", tail_keys, value_heads, preferred_element_type=jnp.float32
    )
    head_queries = jnp.where(first_rows[:, None, None], query_heads, jnp.zeros_like(query_heads))
    head_state = jnp.einsum(
        "lhd,lhe->hde", head_queries, grad_heads, preferred_element_type=jnp.float32
    )
    empty = (jnp.zeros((head_count, HEAD_DIM, HEAD_DIM), jnp.float32), jnp.zeros((), jnp.float32))
    state_in = prefix((tail_state, has_start), "seq", combine_pair, empty, False)[0]
    grad_in = prefix((head_state, has_start), "seq", combine_pair, empty, True)[0]
    pair_mask = (doc_index[:, None] == doc_index[None, :]) & (order[:, None] >= order[None, :])
    score_qk = jnp.einsum(
        "thd,shd->hts", query_heads, key_heads, preferred_element_type=jnp.float32
    )
    weight_qk = jnp.where(pair_mask[None], score_qk, 0.0).astype(jnp.bfloat16)
    score_gv = jnp.einsum(
        "the,she->hts", grad_heads, value_heads, preferred_element_type=jnp.float32
    )
    weight_gv = jnp.where(pair_mask[None], score_gv, 0.0).astype(jnp.bfloat16)
    high = lax.Precision.HIGHEST
    carry_query = jnp.einsum(
        "hde,the->thd", state_in, grad_heads.astype(jnp.float32), precision=high
    )
    query_local = jnp.einsum(
        "hts,shd->thd", weight_gv, key_heads, preferred_element_type=jnp.float32
    )
    query_out = (
        (query_local + jnp.where(first_rows[:, None, None], carry_query, 0.0))
        .reshape(rows_dev, width)
        .astype(jnp.bfloat16)
    )
    carry_key = jnp.einsum("hde,she->shd", grad_in, value_heads.astype(jnp.float32), precision=high)
    carry_value = jnp.einsum("hde,shd->she", grad_in, key_heads.astype(jnp.float32), precision=high)
    key_local = jnp.einsum(
        "hts,thd->shd", weight_gv, query_heads, preferred_element_type=jnp.float32
    )
    value_local = jnp.einsum(
        "hts,the->she", weight_qk, grad_heads, preferred_element_type=jnp.float32
    )
    key_out = (
        (key_local + jnp.where(last_rows[:, None, None], carry_key, 0.0))
        .reshape(rows_dev, width)
        .astype(jnp.bfloat16)
    )
    value_out = (
        (value_local + jnp.where(last_rows[:, None, None], carry_value, 0.0))
        .reshape(rows_dev, width)
        .astype(jnp.bfloat16)
    )
    query_grad, key_grad, value_grad = (
        lax.all_to_all(query_out, "head", split_axis=0, concat_axis=1, tiled=True),
        lax.all_to_all(key_out, "head", split_axis=0, concat_axis=1, tiled=True),
        lax.all_to_all(value_out, "head", split_axis=0, concat_axis=1, tiled=True),
    )
    return (query_grad, key_grad, value_grad)


def solution(mesh):
    return jax.shard_map(
        shards,
        mesh=mesh,
        in_specs=(P("seq", "head"), P("seq", "head"), P("seq", "head"), P("seq", "head"), P()),
        out_specs=(P(("seq", "head"), None), P(("seq", "head"), None), P(("seq", "head"), None)),
        check_vma=False,
    )
```

profile of v0, /device:TPU:504, one launch (start us, length us, event | category | flops | bytes accessed | tf_op | source)
XLA Modules:
  0.0 571.6 jit_solution(11400370984947687798)
XLA Ops:
  9.7 1.1 copy.137
  12.4 1.1 copy.136
  14.1 1.9 fusion.16
  16.7 1.3 dynamic-slice
  18.7 139.0 %all-reduce = f32[64]{0:T(128)S(1)} all-reduce(f32[64]{0:T(128)S(1)} %dynamic-update-slice), channel_id=1, replica_groups=mesh['seq'=64,'head'=8] {'seq'}, use_global_device_ids=true, to_apply=%add | all-reduce | flops 64 | bytes 512
  157.8 1.2 fusion
  159.7 40.7 %all-gather.7.cloned.1.call-done = f32[256,128,128]{2,1,0:T(8,128)} async-done(((f32[4,128,128]{2,1,0:T(8,128)}), f32[256,128,128]{2,1,0:T(8,128)}) %all-gather.7.cloned.1.call-update) | async-done | bytes 16777232 | tf_op jit(solution)/shard_map/all_gather | solution.py:13
  202.5 4.2 all-to-all-start.2
  206.8 187.3 %all-gather.5.cloned.1.call-done = f32[256,128,128]{2,1,0:T(8,128)} async-done(((f32[4,128,128]{2,1,0:T(8,128)}), f32[256,128,128]{2,1,0:T(8,128)}) %all-gather.5.cloned.1.call-update) | async-done | bytes 16777232 | tf_op jit(solution)/shard_map/all_gather | solution.py:13
  394.1 145.8 %while.26 = (s32[]{:T(128)}, f32[4,128,128]{2,1,0:T(8,128)S(1)}, s32[]{:T(128)}, f32[64,4,128,128]{3,2,1,0:T(8,128)}, f32[64]{0:T(128)S(1)}, /*index=5*/s32[]{:T(128)}, s32[]{:T(128)}, s32[]{:T(128)}, f32[1]{0:T(128)}) while((s32[]{:T(128)}, f32[4,128,128]{2,1,0:T(8,128)S(1)}, s32[]{:T(128)}, f32[64,4,128,128]{3,2,1,0:T(8,128)}, ...), condition=%wide.region_5.6_spmd, body=%wide.region_4.5_spmd.sunk | while | flops 131078 | bytes 786591 | solution.py:22
  395.3 1.0 bitcast_add_fusion.4
  397.7 1.0 bitcast_add_fusion.4
  400.0 1.0 bitcast_add_fusion.4
  402.3 1.0 bitcast_add_fusion.4
  409.2 1.0 bitcast_add_fusion.4
  411.6 1.0 bitcast_add_fusion.4
  413.9 1.0 bitcast_add_fusion.4
  416.2 1.0 bitcast_add_fusion.4
  423.1 1.0 bitcast_add_fusion.4
  425.4 1.0 bitcast_add_fusion.4
  541.4 4.3 all-to-all-start
  547.0 6.1 %all-to-all-done = bf16[8,32,512]{2,1,0:T(8,128)(2,1)S(1)} async-done(((bf16[8,32,512]{2,1,0:T(8,128)(2,1)}), bf16[8,32,512]{2,1,0:T(8,128)(2,1)S(1)}, u32[]{:S(2)}, u32[]{:S(2)}) %all-to-all-start) | async-done | bytes 262176 | tf_op jit(solution)/shard_map/all_to_all | solution.py:98
  553.1 3.4 all-to-all-start.1
  558.0 6.0 %all-to-all-done.1 = bf16[8,32,512]{2,1,0:T(8,128)(2,1)S(1)} async-done(((bf16[8,32,512]{2,1,0:T(8,128)(2,1)}), bf16[8,32,512]{2,1,0:T(8,128)(2,1)S(1)}, u32[]{:S(2)}, u32[]{:S(2)}) %all-to-all-start.1) | async-done | bytes 262176 | tf_op jit(solution)/shard_map/all_to_all | solution.py:99
  (157 shorter events, 105.8 us)
Async XLA Ops:
  7.2 3.6 copy-start
  7.2 538.4 %copy-start.1 = (bf16[256,512]{1,0:T(8,128)(2,1)S(1)}, bf16[256,512]{1,0:T(8,128)(2,1)}, u32[]{:S(2)}) copy-start(bf16[256,512]{1,0:T(8,128)(2,1)} %param.11) | copy-start | bytes 786436
  7.2 193.3 %all-gather.7.cloned.1.call-start = ((), (), s32[]{:S(2)}) async-start(), calls=%async_computation.4 | async-start | bytes 17039360 | tf_op jit(solution)/shard_map/all_gather | solution.py:13
  11.7 382.4 %all-gather.5.cloned.1.call-start = ((), (), s32[]{:S(2)}) async-start(), calls=%async_computation.3 | async-start | bytes 17039360 | tf_op jit(solution)/shard_map/all_gather | solution.py:13
  202.5 338.8 %all-to-all-start.2 = ((bf16[8,32,512]{2,1,0:T(8,128)(2,1)}), bf16[8,32,512]{2,1,0:T(8,128)(2,1)S(1)}, u32[]{:S(2)}, u32[]{:S(2)}) async-start(bf16[8,32,512]{2,1,0:T(8,128)(2,1)} %convert_element_type.42), calls=%async_computation.2 | async-start | bytes 524288 | tf_op jit(solution)/shard_map/all_to_all | solution.py:100
  541.4 11.8 %all-to-all-start = ((bf16[8,32,512]{2,1,0:T(8,128)(2,1)}), bf16[8,32,512]{2,1,0:T(8,128)(2,1)S(1)}, u32[]{:S(2)}, u32[]{:S(2)}) async-start(bf16[8,32,512]{2,1,0:T(8,128)(2,1)} %convert_element_type.37), calls=%async_computation | async-start | bytes 524288 | tf_op jit(solution)/shard_map/all_to_all | solution.py:98
  553.1 10.9 %all-to-all-start.1 = ((bf16[8,32,512]{2,1,0:T(8,128)(2,1)}), bf16[8,32,512]{2,1,0:T(8,128)(2,1)S(1)}, u32[]{:S(2)}, u32[]{:S(2)}) async-start(bf16[8,32,512]{2,1,0:T(8,128)(2,1)} %convert_element_type.39), calls=%async_computation.1 | async-start | bytes 524288 | tf_op jit(solution)/shard_map/all_to_all | solution.py:99
Sparse Core Ops, SparseCore 0:
  11.8 188.5 all-gather.6
  204.0 190.0 all-gather.4
where the time goes:
time: 575 us; the launch traced here: 572 us
  waiting for transfers between devices  240 us (42%)
  blocking collectives  139 us (24%)
  other arithmetic  68.5 us (12%)
  local copies, waits for them, and re-layouts  47.8 us (8%)
  loops' own time  42.8 us (7%)
  between operations  14.9 us (3%)
  starting transfers between devices  12 us (2%)
  matrix products  6.47 us (1%)
    all_gather x2, waiting for transfers between devices, prefix(): gathered = jax.tree.map(lambda a: lax.all_gather(a, axis), part)  228 us
    unnamed x1, blocking collectives  139 us
    add x63, other arithmetic, combine_pair(): current[0] + (1.0 - current[1]) * earlier[0]  66.1 us
    another operation x2, loops' own time, prefix(): return lax.fori_loop(0, ahead, one, state)  42.8 us
    dynamic_slice x63, local copies, waits for them, and re-layouts, one(): lax.dynamic_index_in_dim(a, source, 0, False)  36.9 us
  transfers between devices with their start and end apart: 5, of which 4 were waited for; matrix products, arithmetic and copies ran while one was open for 21% of the time, Pallas kernels for 0%

commit v1 on v0

v1 whole, which is shorter than its diff:
```python
import jax
import jax.numpy as jnp
from jax import lax
from jax.sharding import PartitionSpec as P

HEAD_DIM = 128
REACH = 4


def make_shards(blocks):
    def shards(queries, keys, values, out_grad, doc_lengths):
        rows_dev = queries.shape[0]
        width = queries.shape[1]
        head_count = width // HEAD_DIM
        block = lax.axis_index("seq")
        shard_begin = block * rows_dev
        ends = jnp.cumsum(doc_lengths)
        starts = ends - doc_lengths
        order = jnp.arange(rows_dev, dtype=jnp.int32)
        position = shard_begin + order
        before = starts[None, :] <= position[:, None]
        doc_index = jnp.sum(before.astype(jnp.int32), axis=1) - 1
        doc_begin = jnp.max(jnp.where(before, starts[None, :], 0), axis=1)
        first_begin = doc_begin[0]
        last_end = jnp.sum(jnp.where(doc_index[rows_dev - 1] == jnp.arange(doc_lengths.shape[0]), ends, 0))
        first_rows = doc_begin < shard_begin
        last_rows = doc_index == doc_index[rows_dev - 1]
        query_heads = queries.reshape(rows_dev, head_count, HEAD_DIM)
        key_heads = keys.reshape(rows_dev, head_count, HEAD_DIM)
        value_heads = values.reshape(rows_dev, head_count, HEAD_DIM)
        grad_heads = out_grad.reshape(rows_dev, head_count, HEAD_DIM)
        tail_keys = jnp.where(last_rows[:, None, None], key_heads, jnp.zeros_like(key_heads))
        tail_state = jnp.einsum(
            "lhd,lhe->hde", tail_keys, value_heads, preferred_element_type=jnp.float32
        ).astype(jnp.bfloat16)
        head_queries = jnp.where(first_rows[:, None, None], query_heads, jnp.zeros_like(query_heads))
        head_state = jnp.einsum(
            "lhd,lhe->hde", head_queries, grad_heads, preferred_element_type=jnp.float32
        ).astype(jnp.bfloat16)
        state_in = jnp.zeros((head_count, HEAD_DIM, HEAD_DIM), jnp.float32)
        grad_in = jnp.zeros((head_count, HEAD_DIM, HEAD_DIM), jnp.float32)
        for j in range(1, REACH + 1):
            came = lax.ppermute(tail_state, "seq", [(i, (i + j) % blocks) for i in range(blocks)])
            use = first_begin < rows_dev * (block - j + 1)
            state_in = state_in + jnp.where(use, came.astype(jnp.float32), 0.0)
            came = lax.ppermute(head_state, "seq", [(i, (i - j) % blocks) for i in range(blocks)])
            use = last_end > rows_dev * (block + j)
            grad_in = grad_in + jnp.where(use, came.astype(jnp.float32), 0.0)
        state_in = state_in.astype(jnp.bfloat16)
        grad_in = grad_in.astype(jnp.bfloat16)
        pair_mask = (doc_index[:, None] == doc_index[None, :]) & (order[:, None] >= order[None, :])
        score_qk = jnp.einsum(
            "thd,shd->hts", query_heads, key_heads, preferred_element_type=jnp.float32
        )
        weight_qk = jnp.where(pair_mask[None], score_qk, 0.0).astype(jnp.bfloat16)
        score_gv = jnp.einsum(
            "the,she->hts", grad_heads, value_heads, preferred_element_type=jnp.float32
        )
        weight_gv = jnp.where(pair_mask[None], score_gv, 0.0).astype(jnp.bfloat16)
        carry_query = jnp.einsum(
            "hde,the->thd", state_in, grad_heads, preferred_element_type=jnp.float32
        )
        query_local = jnp.einsum(
            "hts,shd->thd", weight_gv, key_heads, preferred_element_type=jnp.float32
        )
        query_out = (
            (query_local + jnp.where(first_rows[:, None, None], carry_query, 0.0))
            .reshape(rows_dev, width)
            .astype(jnp.bfloat16)
        )
        carry_key = jnp.einsum("hde,she->shd", grad_in, value_heads, preferred_element_type=jnp.float32)
        carry_value = jnp.einsum("hde,shd->she", grad_in, key_heads, preferred_element_type=jnp.float32)
        key_local = jnp.einsum(
            "hts,thd->shd", weight_gv, query_heads, preferred_element_type=jnp.float32
        )
        value_local = jnp.einsum(
            "hts,the->she", weight_qk, grad_heads, preferred_element_type=jnp.float32
        )
        key_out = (
            (key_local + jnp.where(last_rows[:, None, None], carry_key, 0.0))
            .reshape(rows_dev, width)
            .astype(jnp.bfloat16)
        )
        value_out = (
            (value_local + jnp.where(last_rows[:, None, None], carry_value, 0.0))
            .reshape(rows_dev, width)
            .astype(jnp.bfloat16)
        )
        return (
            lax.all_to_all(query_out, "head", split_axis=0, concat_axis=1, tiled=True),
            lax.all_to_all(key_out, "head", split_axis=0, concat_axis=1, tiled=True),
            lax.all_to_all(value_out, "head", split_axis=0, concat_axis=1, tiled=True),
        )

    return shards


def solution(mesh):
    return jax.shard_map(
        make_shards(mesh.shape["seq"]),
        mesh=mesh,
        in_specs=(P("seq", "head"), P("seq", "head"), P("seq", "head"), P("seq", "head"), P()),
        out_specs=(P(("seq", "head"), None), P(("seq", "head"), None), P(("seq", "head"), None)),
        check_vma=False,
    )
```

time: 575 us -> 88 us (0.15)
  the two profiles are of different devices: /device:TPU:504 before, /device:TPU:1 now
where the time goes in v1:
time: 88 us; the launch traced here: 87.2 us
  starting transfers between devices  50.8 us (58%)
  waiting for transfers between devices  14.8 us (17%)
  local copies, waits for them, and re-layouts  8.35 us (9%)
  between operations  6.31 us (7%)
  matrix products  4.43 us (5%)
  other arithmetic  2.5 us (3%)
    ppermute x4, starting transfers between devices, shards(): lax.ppermute(head_state, 'seq', [(i, (i - j) % blocks) for i in range(blo...  20 us
    ppermute x4, starting transfers between devices, shards(): lax.ppermute(tail_state, 'seq', [(i, (i + j) % blocks) for i in range(blo...  15.2 us
    all_to_all x1, starting transfers between devices, shards(): lax.all_to_all(query_out, 'head', split_axis=0, concat_axis=1, tiled=True)  6.93 us
    all_to_all x1, waiting for transfers between devices, shards(): lax.all_to_all(value_out, 'head', split_axis=0, concat_axis=1, tiled=True)  5.07 us
    all_to_all x1, waiting for transfers between devices, shards(): lax.all_to_all(key_out, 'head', split_axis=0, concat_axis=1, tiled=True)  4.89 us
    all_to_all x1, waiting for transfers between devices, shards(): lax.all_to_all(query_out, 'head', split_axis=0, concat_axis=1, tiled=True)  4.82 us
    all_to_all x1, starting transfers between devices, shards(): lax.all_to_all(key_out, 'head', split_axis=0, concat_axis=1, tiled=True)  4.36 us
    all_to_all x1, starting transfers between devices, shards(): lax.all_to_all(value_out, 'head', split_axis=0, concat_axis=1, tiled=True)  4.36 us
  transfers between devices with their start and end apart: 11, of which 3 were waited for; matrix products, arithmetic and copies ran while one was open for 12% of the time, Pallas kernels for 0%

profile of v1, /device:TPU:1, one launch (start us, length us, event | category | flops | bytes accessed | tf_op | source)
XLA Modules:
  0.0 87.2 jit_solution(12976575084013938100)
XLA Ops:
  1.7 1.1 %copy.109 = bf16[256,512]{0,1:T(8,128)(2,1)S(1)} copy(bf16[256,512]{1,0:T(8,128)(2,1)} %param.6) | data formatting | bytes 524288 | tf_op jit(solution)/shard_map/reshape | solution.py:29
  4.1 0.9 convolution_convert_fusion.1
  5.0 4.4 %collective-permute-start.3 = (bf16[4,128,128]{2,1,0:T(8,128)(2,1)}, bf16[4,128,128]{2,1,0:T(8,128)(2,1)S(1)}, u32[]{:S(2)}, u32[]{:S(2)}) collective-permute-start(bf16[4,128,128]{2,1,0:T(8,128)(2,1)} %convolution_convert_fusion.1), channel_id=1, source_target_pairs={{0,32},{8,40},{16,48},{24,56},{32,64},{40,72},{48,80},{56,88},{64,... | collective-permute-start | bytes 393224 | tf_op jit(solution)/shard_map/ppermute | solution.py:43
  9.4 4.6 %collective-permute-start.2 = (bf16[4,128,128]{2,1,0:T(8,128)(2,1)}, bf16[4,128,128]{2,1,0:T(8,128)(2,1)}, u32[]{:S(2)}, u32[]{:S(2)}) collective-permute-start(bf16[4,128,128]{2,1,0:T(8,128)(2,1)} %convolution_convert_fusion.1), channel_id=1, source_target_pairs={{0,24},{8,32},{16,40},{24,48},{32,56},{40,64},{48,72},{56,80},{64,... | collective-permute-start | bytes 393224 | tf_op jit(solution)/shard_map/ppermute | solution.py:43
  14.0 3.6 %collective-permute-start.1 = (bf16[4,128,128]{2,1,0:T(8,128)(2,1)}, bf16[4,128,128]{2,1,0:T(8,128)(2,1)}, u32[]{:S(2)}, u32[]{:S(2)}) collective-permute-start(bf16[4,128,128]{2,1,0:T(8,128)(2,1)} %convolution_convert_fusion.1), channel_id=1, source_target_pairs={{0,16},{8,24},{16,32},{24,40},{32,48},{40,56},{48,64},{56,72},{64,... | collective-permute-start | bytes 393224 | tf_op jit(solution)/shard_map/ppermute | solution.py:43
  17.7 2.6 %collective-permute-start = (bf16[4,128,128]{2,1,0:T(8,128)(2,1)}, bf16[4,128,128]{2,1,0:T(8,128)(2,1)}, u32[]{:S(2)}, u32[]{:S(2)}) collective-permute-start(bf16[4,128,128]{2,1,0:T(8,128)(2,1)} %convolution_convert_fusion.1), channel_id=1, source_target_pairs={{0,8},{8,16},{16,24},{24,32},{32,40},{40,48},{48,56},{56,64},{64,7... | collective-permute-start | bytes 393224 | tf_op jit(solution)/shard_map/ppermute | solution.py:43
  20.7 7.7 %collective-permute-start.7 = (bf16[4,128,128]{2,1,0:T(8,128)(2,1)S(1)}, bf16[4,128,128]{2,1,0:T(8,128)(2,1)S(1)}, u32[]{:S(2)}, u32[]{:S(2)}) collective-permute-start(bf16[4,128,128]{2,1,0:T(8,128)(2,1)S(1)} %convolution_convert_fusion), channel_id=1, source_target_pairs={{0,480},{8,488},{16,496},{24,504},{32,0},{40,8},{48,16},{56,24},{6... | collective-permute-start | bytes 393224 | tf_op jit(solution)/shard_map/ppermute | solution.py:46
  29.0 1.4 %fusion.43 = s32[]{:T(128)} fusion(s32[32]{0:T(128)S(1)} %reduce, s32[]{:T(128)} %bitcast.3), kind=kLoop, calls=%fused_computation.59 | loop fusion | flops 95 | bytes 136 | tf_op jit(solution)/shard_map/reduce_sum | solution.py:25
  36.6 4.9 %collective-permute-start.6 = (bf16[4,128,128]{2,1,0:T(8,128)(2,1)S(1)}, bf16[4,128,128]{2,1,0:T(8,128)(2,1)S(1)}, u32[]{:S(2)}, u32[]{:S(2)}) collective-permute-start(bf16[4,128,128]{2,1,0:T(8,128)(2,1)S(1)} %convolution_convert_fusion), channel_id=1, source_target_pairs={{0,488},{8,496},{16,504},{24,0},{32,8},{40,16},{48,24},{56,32},{64... | collective-permute-start | bytes 393224 | tf_op jit(solution)/shard_map/ppermute | solution.py:46
  41.5 4.5 %collective-permute-start.5 = (bf16[4,128,128]{2,1,0:T(8,128)(2,1)S(1)}, bf16[4,128,128]{2,1,0:T(8,128)(2,1)S(1)}, u32[]{:S(2)}, u32[]{:S(2)}) collective-permute-start(bf16[4,128,128]{2,1,0:T(8,128)(2,1)S(1)} %convolution_convert_fusion), channel_id=1, source_target_pairs={{0,496},{8,504},{16,0},{24,8},{32,16},{40,24},{48,32},{56,40},{64,... | collective-permute-start | bytes 393224 | tf_op jit(solution)/shard_map/ppermute | solution.py:46
  46.0 2.9 %collective-permute-start.4 = (bf16[4,128,128]{2,1,0:T(8,128)(2,1)S(1)}, bf16[4,128,128]{2,1,0:T(8,128)(2,1)S(1)}, u32[]{:S(2)}, u32[]{:S(2)}) collective-permute-start(bf16[4,128,128]{2,1,0:T(8,128)(2,1)S(1)} %convolution_convert_fusion), channel_id=1, source_target_pairs={{0,504},{8,0},{16,8},{24,16},{32,24},{40,32},{48,40},{56,48},{64,5... | collective-permute-start | bytes 393224 | tf_op jit(solution)/shard_map/ppermute | solution.py:46
  49.0 1.3 %fusion.11 = bf16[256,4,128]{2,0,1:T(8,128)(2,1)S(1)} fusion(f32[256,4,128]{2,0,1:T(8,128)S(1)} %convolution_bitcast_fusion.1, pred[256]{0:T(512)(128)(4,1)S(1)} %broadcast_compare_fusion.1, bf16[4,128,128]{2,1,0:T(8,128)(2,1)S(1)} %collective-permute-done.3, bf16[4,128,128]{2,1,0:T(8,128)(2,1)} %collective-permute-done.2, ...), kind=kOutput, calls=%fused_computation.18 | convolution fusion | flops 34734080 | bytes 1573124 | tf_op jit(solution)/shard_map/hde,the->thd/dot_general | solution.py:60
  50.5 0.8 convert_element_type.75
  51.3 6.9 %all-to-all-start = ((bf16[8,32,512]{2,1,0:T(8,128)(2,1)}), bf16[8,32,512]{2,1,0:T(8,128)(2,1)S(1)}, u32[]{:S(2)}, u32[]{:S(2)}) async-start(bf16[8,32,512]{2,1,0:T(8,128)(2,1)} %convert_element_type.75), calls=%async_computation | async-start | bytes 524288 | tf_op jit(solution)/shard_map/all_to_all | solution.py:90
  58.8 0.8 convert_element_type.83
  59.9 4.8 %all-to-all-done = bf16[8,32,512]{2,1,0:T(8,128)(2,1)S(1)} async-done(((bf16[8,32,512]{2,1,0:T(8,128)(2,1)}), bf16[8,32,512]{2,1,0:T(8,128)(2,1)S(1)}, u32[]{:S(2)}, u32[]{:S(2)}) %all-to-all-start) | async-done | bytes 262176 | tf_op jit(solution)/shard_map/all_to_all | solution.py:90
  64.7 4.4 %all-to-all-start.1 = ((bf16[8,32,512]{2,1,0:T(8,128)(2,1)}), bf16[8,32,512]{2,1,0:T(8,128)(2,1)S(1)}, u32[]{:S(2)}, u32[]{:S(2)}) async-start(bf16[8,32,512]{2,1,0:T(8,128)(2,1)} %convert_element_type.83), calls=%async_computation.1 | async-start | bytes 524288 | tf_op jit(solution)/shard_map/all_to_all | solution.py:91
  69.9 0.8 convert_element_type.86
  70.7 4.9 %all-to-all-done.1 = bf16[8,32,512]{2,1,0:T(8,128)(2,1)S(1)} async-done(((bf16[8,32,512]{2,1,0:T(8,128)(2,1)}), bf16[8,32,512]{2,1,0:T(8,128)(2,1)S(1)}, u32[]{:S(2)}, u32[]{:S(2)}) %all-to-all-start.1) | async-done | bytes 262176 | tf_op jit(solution)/shard_map/all_to_all | solution.py:91
  75.6 4.4 %all-to-all-start.2 = ((bf16[8,32,512]{2,1,0:T(8,128)(2,1)}), bf16[8,32,512]{2,1,0:T(8,128)(2,1)S(1)}, u32[]{:S(2)}, u32[]{:S(2)}) async-start(bf16[8,32,512]{2,1,0:T(8,128)(2,1)} %convert_element_type.86), calls=%async_computation.2 | async-start | bytes 524288 | tf_op jit(solution)/shard_map/all_to_all | solution.py:92
  80.0 0.7 copy.113
  80.7 0.7 copy.114
  81.4 5.1 %all-to-all-done.2 = bf16[8,32,512]{2,1,0:T(8,128)(2,1)S(1)} async-done(((bf16[8,32,512]{2,1,0:T(8,128)(2,1)}), bf16[8,32,512]{2,1,0:T(8,128)(2,1)S(1)}, u32[]{:S(2)}, u32[]{:S(2)}) %all-to-all-start.2) | async-done | bytes 262176 | tf_op jit(solution)/shard_map/all_to_all | solution.py:92
  86.5 0.7 copy.115
  (40 shorter events, 6.1 us)
Async XLA Ops:
  0.6 19.8 %copy-start = (bf16[256,512]{1,0:T(8,128)(2,1)S(1)}, bf16[256,512]{1,0:T(8,128)(2,1)}, u32[]{:S(2)}) copy-start(bf16[256,512]{1,0:T(8,128)(2,1)} %param.8) | copy-start | bytes 786436
  0.7 0.7 copy-start.3
  1.7 2.4 %copy-start.2 = (bf16[256,512]{1,0:T(8,128)(2,1)S(1)}, bf16[256,512]{1,0:T(8,128)(2,1)}, u32[]{:S(2)}) copy-start(bf16[256,512]{1,0:T(8,128)(2,1)} %param.7) | copy-start | bytes 786436
  4.1 16.1 %copy-start.1 = (bf16[256,512]{1,0:T(8,128)(2,1)S(1)}, bf16[256,512]{1,0:T(8,128)(2,1)}, u32[]{:S(2)}) copy-start(bf16[256,512]{1,0:T(8,128)(2,1)} %param.5) | copy-start | bytes 786436
  5.0 31.6 %collective-permute-start.3 = (bf16[4,128,128]{2,1,0:T(8,128)(2,1)}, bf16[4,128,128]{2,1,0:T(8,128)(2,1)S(1)}, u32[]{:S(2)}, u32[]{:S(2)}) collective-permute-start(bf16[4,128,128]{2,1,0:T(8,128)(2,1)} %convolution_convert_fusion.1), channel_id=1, source_target_pairs={{0,32},{8,40},{16,48},{24,56},{32,64},{40,72},{48,80},{56,88},{64,... | collective-permute-start | bytes 393224 | tf_op jit(solution)/shard_map/ppermute | solution.py:43
  9.4 32.1 %collective-permute-start.2 = (bf16[4,128,128]{2,1,0:T(8,128)(2,1)}, bf16[4,128,128]{2,1,0:T(8,128)(2,1)}, u32[]{:S(2)}, u32[]{:S(2)}) collective-permute-start(bf16[4,128,128]{2,1,0:T(8,128)(2,1)} %convolution_convert_fusion.1), channel_id=1, source_target_pairs={{0,24},{8,32},{16,40},{24,48},{32,56},{40,64},{48,72},{56,80},{64,... | collective-permute-start | bytes 393224 | tf_op jit(solution)/shard_map/ppermute | solution.py:43
  14.0 32.0 %collective-permute-start.1 = (bf16[4,128,128]{2,1,0:T(8,128)(2,1)}, bf16[4,128,128]{2,1,0:T(8,128)(2,1)}, u32[]{:S(2)}, u32[]{:S(2)}) collective-permute-start(bf16[4,128,128]{2,1,0:T(8,128)(2,1)} %convolution_convert_fusion.1), channel_id=1, source_target_pairs={{0,16},{8,24},{16,32},{24,40},{32,48},{40,56},{48,64},{56,72},{64,... | collective-permute-start | bytes 393224 | tf_op jit(solution)/shard_map/ppermute | solution.py:43
  17.7 31.3 %collective-permute-start = (bf16[4,128,128]{2,1,0:T(8,128)(2,1)}, bf16[4,128,128]{2,1,0:T(8,128)(2,1)}, u32[]{:S(2)}, u32[]{:S(2)}) collective-permute-start(bf16[4,128,128]{2,1,0:T(8,128)(2,1)} %convolution_convert_fusion.1), channel_id=1, source_target_pairs={{0,8},{8,16},{16,24},{24,32},{32,40},{40,48},{48,56},{56,64},{64,7... | collective-permute-start | bytes 393224 | tf_op jit(solution)/shard_map/ppermute | solution.py:43
  20.7 37.6 %collective-permute-start.7 = (bf16[4,128,128]{2,1,0:T(8,128)(2,1)S(1)}, bf16[4,128,128]{2,1,0:T(8,128)(2,1)S(1)}, u32[]{:S(2)}, u32[]{:S(2)}) collective-permute-start(bf16[4,128,128]{2,1,0:T(8,128)(2,1)S(1)} %convolution_convert_fusion), channel_id=1, source_target_pairs={{0,480},{8,488},{16,496},{24,504},{32,0},{40,8},{48,16},{56,24},{6... | collective-permute-start | bytes 393224 | tf_op jit(solution)/shard_map/ppermute | solution.py:46
  36.6 21.6 %collective-permute-start.6 = (bf16[4,128,128]{2,1,0:T(8,128)(2,1)S(1)}, bf16[4,128,128]{2,1,0:T(8,128)(2,1)S(1)}, u32[]{:S(2)}, u32[]{:S(2)}) collective-permute-start(bf16[4,128,128]{2,1,0:T(8,128)(2,1)S(1)} %convolution_convert_fusion), channel_id=1, source_target_pairs={{0,488},{8,496},{16,504},{24,0},{32,8},{40,16},{48,24},{56,32},{64... | collective-permute-start | bytes 393224 | tf_op jit(solution)/shard_map/ppermute | solution.py:46
  41.5 16.7 %collective-permute-start.5 = (bf16[4,128,128]{2,1,0:T(8,128)(2,1)S(1)}, bf16[4,128,128]{2,1,0:T(8,128)(2,1)S(1)}, u32[]{:S(2)}, u32[]{:S(2)}) collective-permute-start(bf16[4,128,128]{2,1,0:T(8,128)(2,1)S(1)} %convolution_convert_fusion), channel_id=1, source_target_pairs={{0,496},{8,504},{16,0},{24,8},{32,16},{40,24},{48,32},{56,40},{64,... | collective-permute-start | bytes 393224 | tf_op jit(solution)/shard_map/ppermute | solution.py:46
  46.0 12.2 %collective-permute-start.4 = (bf16[4,128,128]{2,1,0:T(8,128)(2,1)S(1)}, bf16[4,128,128]{2,1,0:T(8,128)(2,1)S(1)}, u32[]{:S(2)}, u32[]{:S(2)}) collective-permute-start(bf16[4,128,128]{2,1,0:T(8,128)(2,1)S(1)} %convolution_convert_fusion), channel_id=1, source_target_pairs={{0,504},{8,0},{16,8},{24,16},{32,24},{40,32},{48,40},{56,48},{64,5... | collective-permute-start | bytes 393224 | tf_op jit(solution)/shard_map/ppermute | solution.py:46
  51.3 13.4 %all-to-all-start = ((bf16[8,32,512]{2,1,0:T(8,128)(2,1)}), bf16[8,32,512]{2,1,0:T(8,128)(2,1)S(1)}, u32[]{:S(2)}, u32[]{:S(2)}) async-start(bf16[8,32,512]{2,1,0:T(8,128)(2,1)} %convert_element_type.75), calls=%async_computation | async-start | bytes 524288 | tf_op jit(solution)/shard_map/all_to_all | solution.py:90
  64.7 10.9 %all-to-all-start.1 = ((bf16[8,32,512]{2,1,0:T(8,128)(2,1)}), bf16[8,32,512]{2,1,0:T(8,128)(2,1)S(1)}, u32[]{:S(2)}, u32[]{:S(2)}) async-start(bf16[8,32,512]{2,1,0:T(8,128)(2,1)} %convert_element_type.83), calls=%async_computation.1 | async-start | bytes 524288 | tf_op jit(solution)/shard_map/all_to_all | solution.py:91
  75.6 10.9 %all-to-all-start.2 = ((bf16[8,32,512]{2,1,0:T(8,128)(2,1)}), bf16[8,32,512]{2,1,0:T(8,128)(2,1)S(1)}, u32[]{:S(2)}, u32[]{:S(2)}) async-start(bf16[8,32,512]{2,1,0:T(8,128)(2,1)} %convert_element_type.86), calls=%async_computation.2 | async-start | bytes 524288 | tf_op jit(solution)/shard_map/all_to_all | solution.py:92

commit v2 on v1

v2 whole, which is shorter than its diff:
```python
import functools

import jax
import jax.numpy as jnp
from jax import lax
from jax.experimental import pallas as pl
from jax.experimental.pallas import tpu as pltpu
from jax.sharding import PartitionSpec as P

HEAD_DIM = 128
MESH = pl.DeviceIdType.MESH
F32 = jnp.float32
BF16 = jnp.bfloat16

NN = (((1,), (0,)), ((), ()))
NT = (((1,), (1,)), ((), ()))
TN = (((0,), (0,)), ((), ()))


def mm(a, b, dims):
    return lax.dot_general(a, b, dims, preferred_element_type=F32)


def kernel(
    blocks, groups,
    q_hbm, k_hbm, v_hbm, g_hbm, len_ref,
    out_ref,
    q_ref, k_ref, v_ref, g_ref, local, own, first, pair, made,
    in_sem, state_send, state_recv, out_send, out_recv, own_sem,
):
    rows, width = q_ref.shape
    heads = width // HEAD_DIM
    rows_out = rows // groups
    b = lax.axis_index("seq")
    h = lax.axis_index("head")

    loads = [
        pltpu.make_async_copy(src, dst, in_sem.at[i])
        for i, (src, dst) in enumerate(((k_hbm, k_ref), (v_hbm, v_ref), (q_hbm, q_ref), (g_hbm, g_ref)))
    ]
    for load in loads:
        load.start()

    shifts = (1, 3, -1, -3)
    neighbours = {s: lax.rem(b + s + blocks, blocks) for s in shifts}
    order = sorted(range(1, groups), key=lambda k: -min(k // 2, (groups - k) // 2))
    peers = {k: lax.rem(h + k, groups) for k in order}

    barrier = pltpu.get_barrier_semaphore()
    for s in shifts:
        pl.semaphore_signal(barrier, inc=1, device_id={"seq": neighbours[s]}, device_id_type=MESH)
    for k in order:
        pl.semaphore_signal(barrier, inc=1, device_id={"head": peers[k]}, device_id_type=MESH)

    docs = len_ref.shape[1]
    begin_block = (b * rows).astype(F32)
    lengths = jnp.broadcast_to(len_ref[...].astype(F32), (docs, docs))
    down = lax.broadcasted_iota(jnp.int32, (docs, docs), 0)
    across = lax.broadcasted_iota(jnp.int32, (docs, docs), 1)
    length_col = jnp.sum(jnp.where(down == across, lengths, 0.0), axis=1, keepdims=True)
    ends = jnp.sum(jnp.where(down <= across, length_col, 0.0), axis=0, keepdims=True)
    starts = ends - lengths[:1]
    far = 1e9
    place = lax.broadcasted_iota(jnp.int32, (rows, docs), 0).astype(F32) + begin_block
    starts_all = jnp.broadcast_to(starts, (rows, docs))
    ends_all = jnp.broadcast_to(ends, (rows, docs))
    doc_begin = jnp.max(jnp.where(starts_all <= place, starts_all, 0.0), axis=1, keepdims=True)
    doc_end = jnp.min(jnp.where(ends_all > place, ends_all, far), axis=1, keepdims=True)
    last_place = begin_block + (rows - 1)
    begin_first = jnp.max(jnp.where(starts <= begin_block, starts, 0.0), axis=1, keepdims=True)
    begin_last = jnp.max(jnp.where(starts <= last_place, starts, 0.0), axis=1, keepdims=True)
    end_last = jnp.min(jnp.where(ends > last_place, ends, far), axis=1, keepdims=True)
    through = (begin_last < begin_block).astype(F32)
    far_before = (begin_first < begin_block - 2 * rows).astype(F32)
    far_after = (end_last > begin_block + 3 * rows).astype(F32)
    first_rows = jnp.broadcast_to((doc_begin < begin_block).astype(F32), (rows, HEAD_DIM)).astype(BF16)
    last_rows = jnp.broadcast_to((doc_end > last_place).astype(F32), (rows, HEAD_DIM)).astype(BF16)
    row = lax.broadcasted_iota(jnp.int32, (rows, rows), 0).astype(F32)
    col = lax.broadcasted_iota(jnp.int32, (rows, rows), 1).astype(F32)
    pair[0] = ((col >= doc_begin - begin_block) & (col <= row)).astype(F32).astype(BF16)
    pair[1] = ((col < doc_end - begin_block) & (col >= row)).astype(F32).astype(BF16)

    def cols(i):
        return pl.ds(i * HEAD_DIM, HEAD_DIM)

    def state_copy(i, way, kind):
        s = ((1, 1, 3), (-1, -1, -3))[way][kind]
        return pltpu.make_async_remote_copy(
            src_ref=first.at[way, min(kind, 1), i],
            dst_ref=first.at[way, 2 + kind, i],
            send_sem=state_send.at[way, kind, i],
            recv_sem=state_recv.at[way, kind, i],
            device_id={"seq": neighbours[s]},
            device_id_type=MESH,
        )

    def out_copy(i, k):
        return pltpu.make_async_remote_copy(
            src_ref=made.at[i, :, pl.ds(pl.multiple_of(peers[k] * rows_out, rows_out), rows_out), :],
            dst_ref=out_ref.at[:, :, pl.ds(pl.multiple_of(h * width + i * HEAD_DIM, HEAD_DIM), HEAD_DIM)],
            send_sem=out_send.at[k, i],
            recv_sem=out_recv.at[k, i],
            device_id={"head": peers[k]},
            device_id_type=MESH,
        )

    def own_copy(i):
        return pltpu.make_async_copy(
            made.at[i, :, pl.ds(pl.multiple_of(h * rows_out, rows_out), rows_out), :],
            out_ref.at[:, :, pl.ds(pl.multiple_of(h * width + i * HEAD_DIM, HEAD_DIM), HEAD_DIM)],
            own_sem.at[i],
        )

    def states(i):
        tail = mm(v_ref[:, cols(i)], k_ref[:, cols(i)] * last_rows, TN)
        own[0, i] = tail
        first[0, 0, i] = tail.astype(BF16)
        head = mm(q_ref[:, cols(i)], g_ref[:, cols(i)] * first_rows, TN)
        own[1, i] = head
        first[1, 0, i] = head.astype(BF16)

    def pass_on(i):
        for way in range(2):
            state_copy(i, way, 0).wait_recv()
            both = own[way, i] + through * first[way, 2, i].astype(F32)
            first[way, 1, i] = both.astype(BF16)
            state_copy(i, way, 1).start()
            state_copy(i, way, 2).start()

    def inner(i):
        q, k, v, g = (ref[:, cols(i)] for ref in (q_ref, k_ref, v_ref, g_ref))
        weight = mm(g, v, NT).astype(BF16) * pair[0]
        local[0, i] = mm(weight, k, NN)
        weight = mm(v, g, NT).astype(BF16) * pair[1]
        local[1, i] = mm(weight, q, NN)
        weight = mm(k, q, NT).astype(BF16) * pair[1]
        local[2, i] = mm(weight, g, NN)

    def whole(way, i, reach):
        state_copy(i, way, 1).wait_recv()
        state_copy(i, way, 2).wait_recv()
        total = first[way, 3, i].astype(F32) + reach * first[way, 4, i].astype(F32)
        high = total.astype(BF16)
        return high, (total - high.astype(F32)).astype(BF16)

    def finish(i):
        high, low = whole(0, i, far_before)
        g = g_ref[:, cols(i)] * first_rows
        made[i, 0] = (local[0, i] + (mm(g, high, NN) + mm(g, low, NN))).astype(BF16)
        high, low = whole(1, i, far_after)
        v = v_ref[:, cols(i)] * last_rows
        made[i, 1] = (local[1, i] + (mm(v, high, NT) + mm(v, low, NT))).astype(BF16)
        k = k_ref[:, cols(i)] * last_rows
        made[i, 2] = (local[2, i] + (mm(k, high, NN) + mm(k, low, NN))).astype(BF16)
        for peer in order:
            out_copy(i, peer).start()
        own_copy(i).start()

    for load in loads:
        load.wait()
    states(0)
    pl.semaphore_wait(barrier, len(shifts) + len(order))
    for i in range(heads):
        if i:
            states(i)
        for way in range(2):
            state_copy(i, way, 0).start()
    half = max(heads // 2, 1)
    for i in range(half):
        inner(i)
    for i in range(half):
        pass_on(i)
    for i in range(half, heads):
        pass_on(i)
        inner(i)
    for i in range(heads):
        finish(i)
    for i in range(heads):
        own_copy(i).wait()
        for way in range(2):
            for kind in range(3):
                state_copy(i, way, kind).wait_send()
        for k in order:
            out_copy(i, k).wait()


def make_shards(blocks, groups):
    def shards(queries, keys, values, out_grad, doc_lengths):
        rows, width = queries.shape
        heads = width // HEAD_DIM
        rows_out = rows // groups
        out = pl.pallas_call(
            functools.partial(kernel, blocks, groups),
            out_shape=jax.ShapeDtypeStruct((3, rows_out, width * groups), BF16),
            in_specs=[pl.BlockSpec(memory_space=pl.ANY)] * 4 + [pl.BlockSpec(memory_space=pltpu.VMEM)],
            out_specs=pl.BlockSpec(memory_space=pltpu.VMEM),
            scratch_shapes=[pltpu.VMEM((rows, width), BF16)] * 4
            + [
                pltpu.VMEM((3, heads, rows, HEAD_DIM), F32),
                pltpu.VMEM((2, heads, HEAD_DIM, HEAD_DIM), F32),
                pltpu.VMEM((2, 5, heads, HEAD_DIM, HEAD_DIM), BF16),
                pltpu.VMEM((2, rows, rows), BF16),
                pltpu.VMEM((heads, 3, rows, HEAD_DIM), BF16),
                pltpu.SemaphoreType.DMA((4,)),
                pltpu.SemaphoreType.DMA((2, 3, heads)),
                pltpu.SemaphoreType.DMA((2, 3, heads)),
                pltpu.SemaphoreType.DMA((groups, heads)),
                pltpu.SemaphoreType.DMA((groups, heads)),
                pltpu.SemaphoreType.DMA((heads,)),
            ],
            compiler_params=pltpu.CompilerParams(collective_id=0, has_side_effects=True),
        )(queries, keys, values, out_grad, doc_lengths.reshape(1, -1))
        return out[0], out[1], out[2]

    return shards


def solution(mesh):
    return jax.shard_map(
        make_shards(mesh.shape["seq"], mesh.shape["head"]),
        mesh=mesh,
        in_specs=(P("seq", "head"), P("seq", "head"), P("seq", "head"), P("seq", "head"), P()),
        out_specs=(P(("seq", "head"), None), P(("seq", "head"), None), P(("seq", "head"), None)),
        check_vma=False,
    )
```

time: 88 us -> 37.7 us (0.43)
  starting transfers between devices: 50.8 us -> 0 us
  Pallas kernels: 0 us -> 34.9 us
  waiting for transfers between devices: 14.8 us -> 0 us
  local copies, waits for them, and re-layouts: 8.35 us -> 2 us
  between operations: 6.31 us -> 0.64 us
  matrix products: 4.43 us -> 0 us
  other arithmetic: 2.5 us -> 0 us
    ppermute x8 -> x0, starting transfers between devices: 35.2 us -> none  [the longest x4 20 us: shards(): lax.ppermute(head_state, 'seq', [(i, (i - j) % blocks) for i in range(blo...]
    pallas_call x0 -> x1, Pallas kernels: none -> 34.9 us  [shards(): pl.pallas_call(functools.partial(kernel, blocks, groups), out_shape=jax.S...]
    all_to_all x3 -> x0, starting transfers between devices: 15.6 us -> none  [the longest x1 6.93 us: shards(): lax.all_to_all(query_out, 'head', split_axis=0, concat_axis=1, tiled=True)]
    all_to_all x3 -> x0, waiting for transfers between devices: 14.8 us -> none  [the longest x1 5.07 us: shards(): lax.all_to_all(value_out, 'head', split_axis=0, concat_axis=1, tiled=True)]
    dot_general x9 -> x0, matrix products: 4.43 us -> none  [the longest x1 1.31 us: shards(): jnp.einsum('hde,the->thd', state_in, grad_heads, preferred_element_type=j...]
    convert_element_type x6 -> x0, local copies, waits for them, and re-layouts: 3.03 us -> none  [the longest x2 1.01 us: shards(): query_out = (query_local + jnp.where(first_rows[:, None, None], carry_que...]
    all_to_all x3 -> x0, local copies, waits for them, and re-layouts: 2.17 us -> none  [the longest x1 0.72 us: shards(): lax.all_to_all(value_out, 'head', split_axis=0, concat_axis=1, tiled=True)]
    squeeze x0 -> x1, local copies, waits for them, and re-layouts: none -> 2 us  [shards(): return (out[0], out[1], out[2])]
  transfers between devices with their start and end apart: 11 -> 0, of which waited for: 3 -> 0; matrix products, arithmetic and copies ran while one was open for 12% -> 0% of each run, Pallas kernels for 0% -> 0%
where the time goes in v2:
time: 37.7 us; the launch traced here: 37.5 us
  Pallas kernels  34.9 us (93%)
  local copies, waits for them, and re-layouts  2 us (5%)
  between operations  0.64 us (2%)
    pallas_call x1, Pallas kernels, shards(): pl.pallas_call(functools.partial(kernel, blocks, groups), out_shape=jax.S...  34.9 us
    squeeze x1, local copies, waits for them, and re-layouts, shards(): return (out[0], out[1], out[2])  2 us

profile of v2, /device:TPU:1, one launch (start us, length us, event | category | flops | bytes accessed | tf_op | source)
XLA Modules:
  0.0 37.5 jit_solution(10277279215189987970)
XLA Ops:
  0.6 34.9 %shard_map.76 = bf16[3,32,4096]{2,1,0:T(8,128)(2,1)} custom-call(bf16[256,512]{1,0:T(8,128)(2,1)} %q_hbm.1, bf16[256,512]{1,0:T(8,128)(2,1)} %k_hbm.1, bf16[256,512]{1,0:T(8,128)(2,1)} %v_hbm.1, bf16[256,512]{1,0:T(8,128)(2,1)} %g_hbm.1, s32[1,32]{1,0:T(1,128)} %bitcast.7), custom_call_target="tpu_custom_call" | custom-call | tf_op jit(solution)/shard_map/pallas_call | solution.py:192
  35.5 2.0 %slice_bitcast_fusion = (bf16[32,4096]{1,0:T(8,128)(2,1)}, bf16[32,4096]{1,0:T(8,128)(2,1)}, bf16[32,4096]{1,0:T(8,128)(2,1)}) fusion(bf16[3,32,4096]{2,1,0:T(8,128)(2,1)} %shard_map.76), kind=kLoop, calls=%fused_computation | loop fusion | bytes 1572864 | tf_op jit(solution)/shard_map/squeeze | solution.py:213

commit v3 on v2

--- a/solution.py
+++ b/solution.py
@@ -42,13 +42,15 @@
         load.start()
 
     shifts = (1, 3, -1, -3)
-    neighbours = {s: lax.rem(b + s + blocks, blocks) for s in shifts}
+    inside = {s: b + s < blocks if s > 0 else b + s >= 0 for s in shifts}
     order = sorted(range(1, groups), key=lambda k: -min(k // 2, (groups - k) // 2))
     peers = {k: lax.rem(h + k, groups) for k in order}
 
     barrier = pltpu.get_barrier_semaphore()
     for s in shifts:
-        pl.semaphore_signal(barrier, inc=1, device_id={"seq": neighbours[s]}, device_id_type=MESH)
+        @pl.when(inside[s])
+        def _():
+            pl.semaphore_signal(barrier, inc=1, device_id={"seq": b + s}, device_id_type=MESH)
     for k in order:
         pl.semaphore_signal(barrier, inc=1, device_id={"head": peers[k]}, device_id_type=MESH)
 
@@ -75,10 +77,18 @@
     far_after = (end_last > begin_block + 3 * rows).astype(F32)
     first_rows = jnp.broadcast_to((doc_begin < begin_block).astype(F32), (rows, HEAD_DIM)).astype(BF16)
     last_rows = jnp.broadcast_to((doc_end > last_place).astype(F32), (rows, HEAD_DIM)).astype(BF16)
-    row = lax.broadcasted_iota(jnp.int32, (rows, rows), 0).astype(F32)
-    col = lax.broadcasted_iota(jnp.int32, (rows, rows), 1).astype(F32)
-    pair[0] = ((col >= doc_begin - begin_block) & (col <= row)).astype(F32).astype(BF16)
-    pair[1] = ((col < doc_end - begin_block) & (col >= row)).astype(F32).astype(BF16)
+
+    def pairs():
+        row = lax.broadcasted_iota(jnp.int32, (rows, rows), 0).astype(F32)
+        col = lax.broadcasted_iota(jnp.int32, (rows, rows), 1).astype(F32)
+        pair[0] = ((col >= doc_begin - begin_block) & (col <= row)).astype(F32).astype(BF16)
+        pair[1] = ((col < doc_end - begin_block) & (col >= row)).astype(F32).astype(BF16)
+
+    for way in range(2):
+        for kind in range(3):
+            @pl.when(jnp.logical_not(inside[((-1, -1, -3), (1, 1, 3))[way][kind]]))
+            def _():
+                first[way, 2 + kind] = jnp.zeros(first.shape[2:], BF16)
 
     def cols(i):
         return pl.ds(i * HEAD_DIM, HEAD_DIM)
@@ -90,9 +100,15 @@
             dst_ref=first.at[way, 2 + kind, i],
             send_sem=state_send.at[way, kind, i],
             recv_sem=state_recv.at[way, kind, i],
-            device_id={"seq": neighbours[s]},
+            device_id={"seq": b + s},
             device_id_type=MESH,
         )
+
+    def to(way, kind):
+        return inside[((1, 1, 3), (-1, -1, -3))[way][kind]]
+
+    def came(way, kind):
+        return inside[((-1, -1, -3), (1, 1, 3))[way][kind]]
 
     def out_copy(i, k):
         return pltpu.make_async_remote_copy(
@@ -119,13 +135,23 @@
         own[1, i] = head
         first[1, 0, i] = head.astype(BF16)
 
+    def send_own(i):
+        for way in range(2):
+            @pl.when(to(way, 0))
+            def _():
+                state_copy(i, way, 0).start()
+
     def pass_on(i):
         for way in range(2):
-            state_copy(i, way, 0).wait_recv()
+            @pl.when(came(way, 0))
+            def _():
+                state_copy(i, way, 0).wait_recv()
             both = own[way, i] + through * first[way, 2, i].astype(F32)
             first[way, 1, i] = both.astype(BF16)
-            state_copy(i, way, 1).start()
-            state_copy(i, way, 2).start()
+            for kind in (1, 2):
+                @pl.when(to(way, kind))
+                def _():
+                    state_copy(i, way, kind).start()
 
     def inner(i):
         q, k, v, g = (ref[:, cols(i)] for ref in (q_ref, k_ref, v_ref, g_ref))
@@ -136,14 +162,20 @@
         weight = mm(k, q, NT).astype(BF16) * pair[1]
         local[2, i] = mm(weight, g, NN)
 
+    def arrive(i):
+        for way in range(2):
+            for kind in (1, 2):
+                @pl.when(came(way, kind))
+                def _():
+                    state_copy(i, way, kind).wait_recv()
+
     def whole(way, i, reach):
-        state_copy(i, way, 1).wait_recv()
-        state_copy(i, way, 2).wait_recv()
         total = first[way, 3, i].astype(F32) + reach * first[way, 4, i].astype(F32)
         high = total.astype(BF16)
         return high, (total - high.astype(F32)).astype(BF16)
 
     def finish(i):
+        arrive(i)
         high, low = whole(0, i, far_before)
         g = g_ref[:, cols(i)] * first_rows
         made[i, 0] = (local[0, i] + (mm(g, high, NN) + mm(g, low, NN))).astype(BF16)
@@ -159,12 +191,12 @@
     for load in loads:
         load.wait()
     states(0)
-    pl.semaphore_wait(barrier, len(shifts) + len(order))
-    for i in range(heads):
-        if i:
-            states(i)
-        for way in range(2):
-            state_copy(i, way, 0).start()
+    pl.semaphore_wait(barrier, len(order) + sum(inside[s].astype(jnp.int32) for s in shifts))
+    send_own(0)
+    for i in range(1, heads):
+        states(i)
+        send_own(i)
+    pairs()
     half = max(heads // 2, 1)
     for i in range(half):
         inner(i)
@@ -179,9 +211,22 @@
         own_copy(i).wait()
         for way in range(2):
             for kind in range(3):
-                state_copy(i, way, kind).wait_send()
+                @pl.when(to(way, kind))
+                def _():
+                    state_copy(i, way, kind).wait_send()
         for k in order:
             out_copy(i, k).wait()
+
+
+def split(whole_ref, a_ref, b_ref, c_ref, sem):
+    copies = [
+        pltpu.make_async_copy(whole_ref.at[i], part, sem.at[i])
+        for i, part in enumerate((a_ref, b_ref, c_ref))
+    ]
+    for copy in copies:
+        copy.start()
+    for copy in copies:
+        copy.wait()
 
 
 def make_shards(blocks, groups):
@@ -191,8 +236,8 @@
         rows_out = rows // groups
         out = pl.pallas_call(
             functools.partial(kernel, blocks, groups),
-            out_shape=jax.ShapeDtypeStruct((3, rows_out, width * groups), BF16),
-            in_specs=[pl.BlockSpec(memory_space=pl.ANY)] * 4 + [pl.BlockSpec(memory_space=pltpu.VMEM)],
+            out_shape=pltpu.VMEM((3, rows_out, width * groups), BF16),
+            in_specs=[pl.BlockSpec(memory_space=pltpu.HBM)] * 4 + [pl.BlockSpec(memory_space=pltpu.VMEM)],
             out_specs=pl.BlockSpec(memory_space=pltpu.VMEM),
             scratch_shapes=[pltpu.VMEM((rows, width), BF16)] * 4
             + [
@@ -208,9 +253,19 @@
                 pltpu.SemaphoreType.DMA((groups, heads)),
                 pltpu.SemaphoreType.DMA((heads,)),
             ],
-            compiler_params=pltpu.CompilerParams(collective_id=0, has_side_effects=True),
+            compiler_params=pltpu.CompilerParams(
+                collective_id=0, has_side_effects=True
+            ),
         )(queries, keys, values, out_grad, doc_lengths.reshape(1, -1))
-        return out[0], out[1], out[2]
+        part = jax.ShapeDtypeStruct((rows_out, width * groups), BF16)
+        return pl.pallas_call(
+            split,
+            out_shape=(part, part, part),
+            in_specs=[pl.BlockSpec(memory_space=pltpu.VMEM)],
+            out_specs=(pl.BlockSpec(memory_space=pl.ANY),) * 3,
+            scratch_shapes=[pltpu.SemaphoreType.DMA((3,))],
+            compiler_params=pltpu.CompilerParams(vmem_limit_bytes=8 << 20),
+        )(out)
 
     return shards
 

time: 37.7 us -> 29.6 us (0.79)
  the two profiles are of different devices: /device:TPU:1 before, /device:TPU:9 now
where the time goes in v3:
time: 29.6 us; the launch traced here: 29.5 us
  Pallas kernels  28.8 us (97%)
  between operations  0.64 us (2%)
    pallas_call x1, Pallas kernels, shards(): pl.pallas_call(functools.partial(kernel, blocks, groups), out_shape=pltpu...  27.9 us
    pallas_call x1, Pallas kernels, shards(): pl.pallas_call(split, out_shape=(part, part, part), in_specs=[pl.BlockSpe...  0.9 us

profile of v3, /device:TPU:9, one launch (start us, length us, event | category | flops | bytes accessed | tf_op | source)
XLA Modules:
  0.0 29.5 jit_solution(13132829654902965961)
XLA Ops:
  0.6 27.9 %shard_map.76.whole_ref = bf16[3,32,4096]{2,1,0:T(8,128)(2,1)S(1)} custom-call(bf16[256,512]{1,0:T(8,128)(2,1)} %q_hbm.1, bf16[256,512]{1,0:T(8,128)(2,1)} %k_hbm.1, bf16[256,512]{1,0:T(8,128)(2,1)} %v_hbm.1, bf16[256,512]{1,0:T(8,128)(2,1)} %g_hbm.1, s32[1,32]{1,0:T(1,128)} %bitcast.1), custom_call_target="tpu_custom_call" | custom-call | tf_op jit(solution)/shard_map/pallas_call | solution.py:237
  28.6 0.9 %shard_map.77 = (bf16[32,4096]{1,0:T(8,128)(2,1)}, bf16[32,4096]{1,0:T(8,128)(2,1)}, bf16[32,4096]{1,0:T(8,128)(2,1)}) custom-call(bf16[3,32,4096]{2,1,0:T(8,128)(2,1)S(1)} %shard_map.76.whole_ref), custom_call_target="tpu_custom_call" | custom-call | tf_op jit(solution)/shard_map/pallas_call | solution.py:261

commit v4 on v3

--- a/solution.py
+++ b/solution.py
@@ -23,10 +23,10 @@
 
 def kernel(
     blocks, groups,
-    q_hbm, k_hbm, v_hbm, g_hbm, len_ref,
+    q_hbm, k_hbm, v_hbm, g_hbm, len_hbm,
     out_ref,
     q_ref, k_ref, v_ref, g_ref, local, own, first, pair, made,
-    in_sem, state_send, state_recv, out_send, out_recv, own_sem,
+    len_ref, table_sem, in_sem, state_send, state_recv, out_send, out_recv, own_sem,
 ):
     rows, width = q_ref.shape
     heads = width // HEAD_DIM
@@ -34,11 +34,19 @@
     b = lax.axis_index("seq")
     h = lax.axis_index("head")
 
+    def cols(i):
+        return pl.ds(i * HEAD_DIM, HEAD_DIM)
+
+    table_load = pltpu.make_async_copy(len_hbm, len_ref, table_sem)
     loads = [
-        pltpu.make_async_copy(src, dst, in_sem.at[i])
-        for i, (src, dst) in enumerate(((k_hbm, k_ref), (v_hbm, v_ref), (q_hbm, q_ref), (g_hbm, g_ref)))
+        [
+            pltpu.make_async_copy(src.at[:, cols(i)], dst.at[:, cols(i)], in_sem.at[n, i])
+            for n, (src, dst) in enumerate(((k_hbm, k_ref), (v_hbm, v_ref), (q_hbm, q_ref), (g_hbm, g_ref)))
+        ]
+        for i in range(heads)
     ]
-    for load in loads:
+    table_load.start()
+    for load in loads[0]:
         load.start()
 
     shifts = (1, 3, -1, -3)
@@ -53,6 +61,10 @@
             pl.semaphore_signal(barrier, inc=1, device_id={"seq": b + s}, device_id_type=MESH)
     for k in order:
         pl.semaphore_signal(barrier, inc=1, device_id={"head": peers[k]}, device_id_type=MESH)
+
+    for load in sum(loads[1:], []):
+        load.start()
+    table_load.wait()
 
     docs = len_ref.shape[1]
     begin_block = (b * rows).astype(F32)
@@ -90,9 +102,6 @@
             def _():
                 first[way, 2 + kind] = jnp.zeros(first.shape[2:], BF16)
 
-    def cols(i):
-        return pl.ds(i * HEAD_DIM, HEAD_DIM)
-
     def state_copy(i, way, kind):
         s = ((1, 1, 3), (-1, -1, -3))[way][kind]
         return pltpu.make_async_remote_copy(
@@ -188,12 +197,14 @@
             out_copy(i, peer).start()
         own_copy(i).start()
 
-    for load in loads:
+    for load in loads[0]:
         load.wait()
     states(0)
     pl.semaphore_wait(barrier, len(order) + sum(inside[s].astype(jnp.int32) for s in shifts))
     send_own(0)
     for i in range(1, heads):
+        for load in loads[i]:
+            load.wait()
         states(i)
         send_own(i)
     pairs()
@@ -234,10 +245,11 @@
         rows, width = queries.shape
         heads = width // HEAD_DIM
         rows_out = rows // groups
+        docs = doc_lengths.shape[0]
         out = pl.pallas_call(
             functools.partial(kernel, blocks, groups),
             out_shape=pltpu.VMEM((3, rows_out, width * groups), BF16),
-            in_specs=[pl.BlockSpec(memory_space=pltpu.HBM)] * 4 + [pl.BlockSpec(memory_space=pltpu.VMEM)],
+            in_specs=[pl.BlockSpec(memory_space=pltpu.HBM)] * 5,
             out_specs=pl.BlockSpec(memory_space=pltpu.VMEM),
             scratch_shapes=[pltpu.VMEM((rows, width), BF16)] * 4
             + [
@@ -246,7 +258,9 @@
                 pltpu.VMEM((2, 5, heads, HEAD_DIM, HEAD_DIM), BF16),
                 pltpu.VMEM((2, rows, rows), BF16),
                 pltpu.VMEM((heads, 3, rows, HEAD_DIM), BF16),
-                pltpu.SemaphoreType.DMA((4,)),
+                pltpu.VMEM((1, docs), jnp.int32),
+                pltpu.SemaphoreType.DMA,
+                pltpu.SemaphoreType.DMA((4, heads)),
                 pltpu.SemaphoreType.DMA((2, 3, heads)),
                 pltpu.SemaphoreType.DMA((2, 3, heads)),
                 pltpu.SemaphoreType.DMA((groups, heads)),

time: 29.6 us -> 29.2 us (0.986)
  Pallas kernels: 28.8 us -> 28.3 us
    pallas_call x1, Pallas kernels: 27.9 us -> 27.4 us  [shards(): pl.pallas_call(functools.partial(kernel, blocks, groups), out_shape=pltpu...]
where the time goes in v4:
time: 29.2 us; the launch traced here: 29 us
  Pallas kernels  28.3 us (97%)
  between operations  0.64 us (2%)
    pallas_call x1, Pallas kernels, shards(): pl.pallas_call(functools.partial(kernel, blocks, groups), out_shape=pltpu...  27.4 us
    pallas_call x1, Pallas kernels, shards(): pl.pallas_call(split, out_shape=(part, part, part), in_specs=[pl.BlockSpe...  0.9 us

profile of v4, /device:TPU:9, one launch (start us, length us, event | category | flops | bytes accessed | tf_op | source)
XLA Modules:
  0.0 29.0 jit_solution(15841470345198575193)
XLA Ops:
  0.6 27.4 %shard_map.76.whole_ref = bf16[3,32,4096]{2,1,0:T(8,128)(2,1)S(1)} custom-call(bf16[256,512]{1,0:T(8,128)(2,1)} %q_hbm.1, bf16[256,512]{1,0:T(8,128)(2,1)} %k_hbm.1, bf16[256,512]{1,0:T(8,128)(2,1)} %v_hbm.1, bf16[256,512]{1,0:T(8,128)(2,1)} %g_hbm.1, s32[1,32]{1,0:T(1,128)} %bitcast.1), custom_call_target="tpu_custom_call" | custom-call | tf_op jit(solution)/shard_map/pallas_call | solution.py:249
  28.1 0.9 %shard_map.77 = (bf16[32,4096]{1,0:T(8,128)(2,1)}, bf16[32,4096]{1,0:T(8,128)(2,1)}, bf16[32,4096]{1,0:T(8,128)(2,1)}) custom-call(bf16[3,32,4096]{2,1,0:T(8,128)(2,1)S(1)} %shard_map.76.whole_ref), custom_call_target="tpu_custom_call" | custom-call | tf_op jit(solution)/shard_map/pallas_call | solution.py:275

commit v5 on v4

--- a/solution.py
+++ b/solution.py
@@ -26,7 +26,7 @@
     q_hbm, k_hbm, v_hbm, g_hbm, len_hbm,
     out_ref,
     q_ref, k_ref, v_ref, g_ref, local, own, first, pair, made,
-    len_ref, table_sem, in_sem, state_send, state_recv, out_send, out_recv, own_sem,
+    len_ref, table_sem, in_sem, state_send, state_recv, out_send, out_recv, own_sem, late_sem,
 ):
     rows, width = q_ref.shape
     heads = width // HEAD_DIM
@@ -49,6 +49,7 @@
     for load in loads[0]:
         load.start()
 
+    late = (b == 0) & (h == 0)
     shifts = (1, 3, -1, -3)
     inside = {s: b + s < blocks if s > 0 else b + s >= 0 for s in shifts}
     order = sorted(range(1, groups), key=lambda k: -min(k // 2, (groups - k) // 2))
@@ -56,11 +57,38 @@
 
     barrier = pltpu.get_barrier_semaphore()
     for s in shifts:
-        @pl.when(inside[s])
+        @pl.when(inside[s] & jnp.logical_not(late))
         def _():
             pl.semaphore_signal(barrier, inc=1, device_id={"seq": b + s}, device_id_type=MESH)
     for k in order:
-        pl.semaphore_signal(barrier, inc=1, device_id={"head": peers[k]}, device_id_type=MESH)
+        @pl.when(jnp.logical_not(late))
+        def _():
+            pl.semaphore_signal(barrier, inc=1, device_id={"head": peers[k]}, device_id_type=MESH)
+
+    def late_seq(s):
+        return (b + s == 0) & (h == 0)
+
+    def late_head(k):
+        return (b == 0) & (peers[k] == 0)
+
+    def wait_late(there):
+        @pl.when(there)
+        def _():
+            pl.semaphore_wait(late_sem, 1)
+
+    def enter():
+        waits = len(order) + sum(inside[s].astype(jnp.int32) for s in shifts)
+        waits = waits - sum(late_seq(s).astype(jnp.int32) for s in shifts)
+        waits = waits - sum(late_head(k).astype(jnp.int32) for k in order)
+        pl.semaphore_wait(barrier, waits)
+        for s in (1, 3):
+            @pl.when(late)
+            def _():
+                pl.semaphore_signal(late_sem, inc=1, device_id={"seq": b + s}, device_id_type=MESH)
+        for k in order:
+            @pl.when(late)
+            def _():
+                pl.semaphore_signal(late_sem, inc=1, device_id={"head": peers[k]}, device_id_type=MESH)
 
     for load in sum(loads[1:], []):
         load.start()
@@ -96,9 +124,19 @@
         pair[0] = ((col >= doc_begin - begin_block) & (col <= row)).astype(F32).astype(BF16)
         pair[1] = ((col < doc_end - begin_block) & (col >= row)).astype(F32).astype(BF16)
 
+    def to(way, kind):
+        if kind == 0:
+            return (b >= 2, b < blocks - 2)[1 - way]
+        return inside[((1, 1, 3), (-1, -1, -3))[way][kind]]
+
+    def came(way, kind):
+        if kind == 0:
+            return (b >= 1) & (b < blocks - 1)
+        return inside[((-1, -1, -3), (1, 1, 3))[way][kind]]
+
     for way in range(2):
         for kind in range(3):
-            @pl.when(jnp.logical_not(inside[((-1, -1, -3), (1, 1, 3))[way][kind]]))
+            @pl.when(jnp.logical_not(came(way, kind)))
             def _():
                 first[way, 2 + kind] = jnp.zeros(first.shape[2:], BF16)
 
@@ -113,28 +151,24 @@
             device_id_type=MESH,
         )
 
-    def to(way, kind):
-        return inside[((1, 1, 3), (-1, -1, -3))[way][kind]]
-
-    def came(way, kind):
-        return inside[((-1, -1, -3), (1, 1, 3))[way][kind]]
-
-    def out_copy(i, k):
+    def out_copy(i, part, k):
         return pltpu.make_async_remote_copy(
-            src_ref=made.at[i, :, pl.ds(pl.multiple_of(peers[k] * rows_out, rows_out), rows_out), :],
-            dst_ref=out_ref.at[:, :, pl.ds(pl.multiple_of(h * width + i * HEAD_DIM, HEAD_DIM), HEAD_DIM)],
-            send_sem=out_send.at[k, i],
-            recv_sem=out_recv.at[k, i],
+            src_ref=made.at[i, parts[part], pl.ds(pl.multiple_of(peers[k] * rows_out, rows_out), rows_out), :],
+            dst_ref=out_ref.at[parts[part], :, pl.ds(pl.multiple_of(h * width + i * HEAD_DIM, HEAD_DIM), HEAD_DIM)],
+            send_sem=out_send.at[part, k, i],
+            recv_sem=out_recv.at[part, k, i],
             device_id={"head": peers[k]},
             device_id_type=MESH,
         )
 
-    def own_copy(i):
+    def own_copy(i, part):
         return pltpu.make_async_copy(
-            made.at[i, :, pl.ds(pl.multiple_of(h * rows_out, rows_out), rows_out), :],
-            out_ref.at[:, :, pl.ds(pl.multiple_of(h * width + i * HEAD_DIM, HEAD_DIM), HEAD_DIM)],
-            own_sem.at[i],
+            made.at[i, parts[part], pl.ds(pl.multiple_of(h * rows_out, rows_out), rows_out), :],
+            out_ref.at[parts[part], :, pl.ds(pl.multiple_of(h * width + i * HEAD_DIM, HEAD_DIM), HEAD_DIM)],
+            own_sem.at[part, i],
         )
+
+    parts = (pl.ds(0, 1), pl.ds(1, 2))
 
     def states(i):
         tail = mm(v_ref[:, cols(i)], k_ref[:, cols(i)] * last_rows, TN)
@@ -151,13 +185,15 @@
                 state_copy(i, way, 0).start()
 
     def pass_on(i):
-        for way in range(2):
+        for way in (1, 0):
             @pl.when(came(way, 0))
             def _():
                 state_copy(i, way, 0).wait_recv()
             both = own[way, i] + through * first[way, 2, i].astype(F32)
             first[way, 1, i] = both.astype(BF16)
             for kind in (1, 2):
+                if way == 1 and i == 0:
+                    wait_late(late_seq((-1, -3)[kind - 1]))
                 @pl.when(to(way, kind))
                 def _():
                     state_copy(i, way, kind).start()
@@ -171,36 +207,42 @@
         weight = mm(k, q, NT).astype(BF16) * pair[1]
         local[2, i] = mm(weight, g, NN)
 
-    def arrive(i):
-        for way in range(2):
-            for kind in (1, 2):
-                @pl.when(came(way, kind))
-                def _():
-                    state_copy(i, way, kind).wait_recv()
+    def arrive(i, way):
+        for kind in (1, 2):
+            @pl.when(came(way, kind))
+            def _():
+                state_copy(i, way, kind).wait_recv()
 
     def whole(way, i, reach):
         total = first[way, 3, i].astype(F32) + reach * first[way, 4, i].astype(F32)
         high = total.astype(BF16)
         return high, (total - high.astype(F32)).astype(BF16)
 
+    def send_out(i, part):
+        for k in order:
+            if i == 0 and part == 1:
+                wait_late(late_head(k))
+            out_copy(i, part, k).start()
+        own_copy(i, part).start()
+
     def finish(i):
-        arrive(i)
-        high, low = whole(0, i, far_before)
-        g = g_ref[:, cols(i)] * first_rows
-        made[i, 0] = (local[0, i] + (mm(g, high, NN) + mm(g, low, NN))).astype(BF16)
+        arrive(i, 1)
         high, low = whole(1, i, far_after)
         v = v_ref[:, cols(i)] * last_rows
         made[i, 1] = (local[1, i] + (mm(v, high, NT) + mm(v, low, NT))).astype(BF16)
         k = k_ref[:, cols(i)] * last_rows
         made[i, 2] = (local[2, i] + (mm(k, high, NN) + mm(k, low, NN))).astype(BF16)
-        for peer in order:
-            out_copy(i, peer).start()
-        own_copy(i).start()
+        send_out(i, 1)
+        arrive(i, 0)
+        high, low = whole(0, i, far_before)
+        g = g_ref[:, cols(i)] * first_rows
+        made[i, 0] = (local[0, i] + (mm(g, high, NN) + mm(g, low, NN))).astype(BF16)
+        send_out(i, 0)
 
     for load in loads[0]:
         load.wait()
     states(0)
-    pl.semaphore_wait(barrier, len(order) + sum(inside[s].astype(jnp.int32) for s in shifts))
+    enter()
     send_own(0)
     for i in range(1, heads):
         for load in loads[i]:
@@ -219,14 +261,15 @@
     for i in range(heads):
         finish(i)
     for i in range(heads):
-        own_copy(i).wait()
+        for part in range(2):
+            own_copy(i, part).wait()
+            for k in order:
+                out_copy(i, part, k).wait()
         for way in range(2):
             for kind in range(3):
                 @pl.when(to(way, kind))
                 def _():
                     state_copy(i, way, kind).wait_send()
-        for k in order:
-            out_copy(i, k).wait()
 
 
 def split(whole_ref, a_ref, b_ref, c_ref, sem):
@@ -263,9 +306,10 @@
                 pltpu.SemaphoreType.DMA((4, heads)),
                 pltpu.SemaphoreType.DMA((2, 3, heads)),
                 pltpu.SemaphoreType.DMA((2, 3, heads)),
-                pltpu.SemaphoreType.DMA((groups, heads)),
-                pltpu.SemaphoreType.DMA((groups, heads)),
-                pltpu.SemaphoreType.DMA((heads,)),
+                pltpu.SemaphoreType.DMA((2, groups, heads)),
+                pltpu.SemaphoreType.DMA((2, groups, heads)),
+                pltpu.SemaphoreType.DMA((2, heads)),
+                pltpu.SemaphoreType.REGULAR,
             ],
             compiler_params=pltpu.CompilerParams(
                 collective_id=0, has_side_effects=True

time: 29.2 us -> 27.8 us (0.952)
  the two profiles are of different devices: /device:TPU:9 before, /device:TPU:385 now
where the time goes in v5:
time: 27.8 us; the launch traced here: 27.6 us
  Pallas kernels  27 us (97%)
  between operations  0.64 us (2%)
    pallas_call x1, Pallas kernels, shards(): pl.pallas_call(functools.partial(kernel, blocks, groups), out_shape=pltpu...  26 us
    pallas_call x1, Pallas kernels, shards(): pl.pallas_call(split, out_shape=(part, part, part), in_specs=[pl.BlockSpe...  0.9 us

profile of v5, /device:TPU:385, one launch (start us, length us, event | category | flops | bytes accessed | tf_op | source)
XLA Modules:
  0.0 27.6 jit_solution(267054511265701046)
XLA Ops:
  0.6 26.0 %shard_map.76.whole_ref = bf16[3,32,4096]{2,1,0:T(8,128)(2,1)S(1)} custom-call(bf16[256,512]{1,0:T(8,128)(2,1)} %q_hbm.1, bf16[256,512]{1,0:T(8,128)(2,1)} %k_hbm.1, bf16[256,512]{1,0:T(8,128)(2,1)} %v_hbm.1, bf16[256,512]{1,0:T(8,128)(2,1)} %g_hbm.1, s32[1,32]{1,0:T(1,128)} %bitcast.1), custom_call_target="tpu_custom_call" | custom-call | tf_op jit(solution)/shard_map/pallas_call | solution.py:292
  26.7 0.9 %shard_map.77 = (bf16[32,4096]{1,0:T(8,128)(2,1)}, bf16[32,4096]{1,0:T(8,128)(2,1)}, bf16[32,4096]{1,0:T(8,128)(2,1)}) custom-call(bf16[3,32,4096]{2,1,0:T(8,128)(2,1)S(1)} %shard_map.76.whole_ref), custom_call_target="tpu_custom_call" | custom-call | tf_op jit(solution)/shard_map/pallas_call | solution.py:319

commit v6 on v5

v6 whole, which is shorter than its diff:
```python
import functools

import jax
import jax.numpy as jnp
from jax import lax
from jax.experimental import pallas as pl
from jax.experimental.pallas import tpu as pltpu
from jax.sharding import PartitionSpec as P

HEAD_DIM = 128
MESH = pl.DeviceIdType.MESH
F32 = jnp.float32
BF16 = jnp.bfloat16

NN = (((1,), (0,)), ((), ()))
NT = (((1,), (1,)), ((), ()))
TN = (((0,), (0,)), ((), ()))


def mm(a, b, dims):
    return lax.dot_general(a, b, dims, preferred_element_type=F32)


def kernel(
    blocks, groups,
    q_hbm, k_hbm, v_hbm, g_hbm, len_hbm,
    out_ref,
    q_ref, k_ref, v_ref, g_ref, local, own, first, pair, made,
    len_ref, table_sem, in_sem, state_send, state_recv, out_send, out_recv, own_sem, late_sem,
):
    rows, width = q_ref.shape
    heads = width // HEAD_DIM
    rows_out = rows // groups
    b = lax.axis_index("seq")
    h = lax.axis_index("head")

    def cols(i):
        return pl.ds(i * HEAD_DIM, HEAD_DIM)

    table_load = pltpu.make_async_copy(len_hbm, len_ref, table_sem)
    loads = [
        [
            pltpu.make_async_copy(src.at[:, cols(i)], dst.at[:, cols(i)], in_sem.at[i])
            for src, dst in ((k_hbm, k_ref), (v_hbm, v_ref), (q_hbm, q_ref), (g_hbm, g_ref))
        ]
        for i in range(heads)
    ]

    def loaded(i):
        all_four = q_ref.at[:, pl.ds(0, 4 * HEAD_DIM)]
        pltpu.make_async_copy(all_four, all_four, in_sem.at[i]).wait()

    table_load.start()
    for load in loads[0]:
        load.start()

    late = (b == 0) & (h == 0)
    shifts = (1, 3, -1, -3)
    hops = (1, 1, 3)
    inside = {s: b + s < blocks if s > 0 else b + s >= 0 for s in shifts}
    order = sorted(range(1, groups), key=lambda k: -min(k // 2, (groups - k) // 2))
    peers = {k: lax.rem(h + k, groups) for k in order}

    barrier = pltpu.get_barrier_semaphore()

    @pl.when(jnp.logical_not(late))
    def _():
        for k in order:
            pl.semaphore_signal(barrier, inc=1, device_id={"head": peers[k]}, device_id_type=MESH)
        for s in shifts:
            @pl.when(inside[s])
            def _():
                pl.semaphore_signal(barrier, inc=1, device_id={"seq": b + s}, device_id_type=MESH)

    def late_seq(s):
        return (b + s == 0) & (h == 0)

    after_late = (h == 0) & (functools.reduce(jnp.logical_or, [b == s for s in shifts if s > 0]))
    beside_late = (b == 0) & (h != 0)

    def wait_late(there):
        @pl.when(there)
        def _():
            pl.semaphore_wait(late_sem, 1)

    def enter():
        waits = len(order) + sum(inside[s].astype(jnp.int32) for s in shifts)
        waits = waits - (after_late | beside_late).astype(jnp.int32)
        pl.semaphore_wait(barrier, waits)

        @pl.when(late)
        def _():
            for k in order:
                pl.semaphore_signal(late_sem, inc=1, device_id={"head": peers[k]}, device_id_type=MESH)
            for s in shifts:
                if s > 0:
                    pl.semaphore_signal(late_sem, inc=1, device_id={"seq": b + s}, device_id_type=MESH)

    for load in sum(loads[1:], []):
        load.start()
    table_load.wait()

    docs = len_ref.shape[1]
    begin_block = (b * rows).astype(F32)
    lengths = jnp.broadcast_to(len_ref[...].astype(F32), (docs, docs))
    down = lax.broadcasted_iota(jnp.int32, (docs, docs), 0)
    across = lax.broadcasted_iota(jnp.int32, (docs, docs), 1)
    length_col = jnp.sum(jnp.where(down == across, lengths, 0.0), axis=1, keepdims=True)
    ends = jnp.sum(jnp.where(down <= across, length_col, 0.0), axis=0, keepdims=True)
    starts = ends - lengths[:1]
    far = 1e9
    last_place = begin_block + (rows - 1)
    begin_first = jnp.max(jnp.where(starts <= begin_block, starts, 0.0), axis=1, keepdims=True)
    begin_last = jnp.max(jnp.where(starts <= last_place, starts, 0.0), axis=1, keepdims=True)
    begin_next = jnp.min(jnp.where(starts >= begin_block, starts, far), axis=1, keepdims=True)
    end_last = jnp.min(jnp.where(ends > last_place, ends, far), axis=1, keepdims=True)
    through = (begin_last < begin_block).astype(F32)
    reach = [
        (begin_first < begin_block - 2 * rows).astype(F32),
        (end_last > begin_block + 3 * rows).astype(F32),
    ]
    lane_place = lax.broadcasted_iota(jnp.int32, (rows, HEAD_DIM), 0).astype(F32) + begin_block
    first_rows = (lane_place < begin_next).astype(F32).astype(BF16)
    last_rows = (lane_place >= begin_last).astype(F32).astype(BF16)

    same = lax.broadcasted_iota(jnp.int32, (rows, docs), 0).astype(F32) + begin_block
    same = ((same >= starts) & (same < ends)).astype(F32).astype(BF16)
    same = mm(same, same, NT)
    row = lax.broadcasted_iota(jnp.int32, (rows, rows), 0)
    col = lax.broadcasted_iota(jnp.int32, (rows, rows), 1)
    pair[0] = jnp.where(col <= row, same, 0.0).astype(BF16)
    pair[1] = jnp.where(col >= row, same, 0.0).astype(BF16)

    def to(way, kind):
        if kind == 0:
            return (b >= 2, b < blocks - 2)[1 - way]
        return inside[(hops[kind], -hops[kind])[way]]

    def came(way, kind):
        if kind == 0:
            return (b >= 1) & (b < blocks - 1)
        return inside[(-hops[kind], hops[kind])[way]]

    for way in range(2):
        for kind in range(3):
            @pl.when(jnp.logical_not(came(way, kind)))
            def _():
                first[way, 2 + kind] = jnp.zeros(first.shape[2:], BF16)

    def state_copy(i, way, kind):
        return pltpu.make_async_remote_copy(
            src_ref=first.at[way, min(kind, 1), i],
            dst_ref=first.at[way, 2 + kind, i],
            send_sem=state_send.at[way, kind],
            recv_sem=state_recv.at[way, min(kind, 1), i],
            device_id={"seq": b + (hops[kind], -hops[kind])[way]},
            device_id_type=MESH,
        )

    def sent(way, kind):
        return pltpu.make_async_copy(first.at[way, 2 + kind], first.at[way, 2 + kind], state_send.at[way, kind])

    def out_copy(i, part, k):
        return pltpu.make_async_remote_copy(
            src_ref=made.at[i, parts[part], pl.ds(pl.multiple_of(peers[k] * rows_out, rows_out), rows_out), :],
            dst_ref=out_ref.at[parts[part], :, pl.ds(pl.multiple_of(h * width + i * HEAD_DIM, HEAD_DIM), HEAD_DIM)],
            send_sem=out_send,
            recv_sem=out_recv,
            device_id={"head": peers[k]},
            device_id_type=MESH,
        )

    def own_copy(i, part):
        return pltpu.make_async_copy(
            made.at[i, parts[part], pl.ds(pl.multiple_of(h * rows_out, rows_out), rows_out), :],
            out_ref.at[parts[part], :, pl.ds(pl.multiple_of(h * width + i * HEAD_DIM, HEAD_DIM), HEAD_DIM)],
            own_sem,
        )

    parts = (pl.ds(0, 1), pl.ds(1, 2))

    def states(i):
        tail = mm(v_ref[:, cols(i)], k_ref[:, cols(i)] * last_rows, TN)
        own[0, i] = tail
        first[0, 0, i] = tail.astype(BF16)
        head = mm(q_ref[:, cols(i)], g_ref[:, cols(i)] * first_rows, TN)
        own[1, i] = head
        first[1, 0, i] = head.astype(BF16)

    def send_own(i):
        for way in range(2):
            @pl.when(to(way, 0))
            def _():
                state_copy(i, way, 0).start()

    def pass_on(i):
        if i == 0:
            wait_late(after_late)
        for way in (1, 0):
            @pl.when(came(way, 0))
            def _():
                state_copy(i, way, 0).wait_recv()
            both = own[way, i] + through * first[way, 2, i].astype(F32)
            first[way, 1, i] = both.astype(BF16)
            for kind in (1, 2):
                @pl.when(to(way, kind))
                def _():
                    state_copy(i, way, kind).start()

    def inner(i):
        q, k, v, g = (ref[:, cols(i)] for ref in (q_ref, k_ref, v_ref, g_ref))
        weight = mm(g, v, NT).astype(BF16) * pair[0]
        local[0, i] = mm(weight, k, NN)
        weight = mm(v, g, NT).astype(BF16) * pair[1]
        local[1, i] = mm(weight, q, NN)
        weight = mm(k, q, NT).astype(BF16) * pair[1]
        local[2, i] = mm(weight, g, NN)

    def arrive(i, way):
        pair_in = first.at[way, pl.ds(3, 2), i]

        @pl.when(came(way, 2))
        def _():
            pltpu.make_async_copy(pair_in, pair_in, state_recv.at[way, 1, i]).wait()

        @pl.when(came(way, 1) & jnp.logical_not(came(way, 2)))
        def _():
            state_copy(i, way, 1).wait_recv()

    def whole(way, i):
        total = first[way, 3, i].astype(F32) + reach[way] * first[way, 4, i].astype(F32)
        high = total.astype(BF16)
        return high, (total - high.astype(F32)).astype(BF16)

    def send_out(i, part):
        for k in order:
            out_copy(i, part, k).start()
        own_copy(i, part).start()

    def twice(x):
        return jnp.concatenate([x, x], axis=1)

    def keys_values(i):
        high, low = whole(1, i)
        v = v_ref[:, cols(i)] * last_rows
        made[i, 1] = (local[1, i] + (mm(v, high, NT) + mm(v, low, NT))).astype(BF16)
        k = k_ref[:, cols(i)] * last_rows
        both = jnp.concatenate([high, low], axis=0)
        made[i, 2] = (local[2, i] + mm(twice(k), both, NN)).astype(BF16)

    def query(i):
        high, low = whole(0, i)
        g = g_ref[:, cols(i)] * first_rows
        both = jnp.concatenate([high, low], axis=0)
        made[i, 0] = (local[0, i] + mm(twice(g), both, NN)).astype(BF16)

    def finish(i):
        if i == 0:
            wait_late(beside_late)
        arrive(i, 1)
        keys_values(i)
        send_out(i, 1)
        arrive(i, 0)
        query(i)
        send_out(i, 0)

    loaded(0)
    states(0)
    enter()
    send_own(0)
    for i in range(1, heads):
        loaded(i)
        states(i)
        send_own(i)
    half = max(heads // 2, 1)
    for i in range(half):
        inner(i)
    for i in range(heads):
        pass_on(i)
    for i in range(half, heads):
        inner(i)
    for i in range(heads):
        finish(i)
    mine = out_ref.at[:, :, pl.ds(0, width)]
    others = out_ref.at[:, :, pl.ds(0, width * (groups - 1))]
    pltpu.make_async_copy(mine, mine, own_sem).wait()
    for way in range(2):
        for kind in range(3):
            @pl.when(to(way, kind))
            def _():
                sent(way, kind).wait()
    pltpu.make_async_copy(others, others, out_recv).wait()
    pltpu.make_async_copy(others, others, out_send).wait()


def split(whole_ref, a_ref, b_ref, c_ref, sem):
    copies = [
        pltpu.make_async_copy(whole_ref.at[i], part, sem.at[i])
        for i, part in enumerate((a_ref, b_ref, c_ref))
    ]
    for copy in copies:
        copy.start()
    for copy in copies:
        copy.wait()


def make_shards(blocks, groups):
    def shards(queries, keys, values, out_grad, doc_lengths):
        rows, width = queries.shape
        heads = width // HEAD_DIM
        rows_out = rows // groups
        docs = doc_lengths.shape[0]
        out = pl.pallas_call(
            functools.partial(kernel, blocks, groups),
            out_shape=pltpu.VMEM((3, rows_out, width * groups), BF16),
            in_specs=[pl.BlockSpec(memory_space=pltpu.HBM)] * 5,
            out_specs=pl.BlockSpec(memory_space=pltpu.VMEM),
            scratch_shapes=[pltpu.VMEM((rows, width), BF16)] * 4
            + [
                pltpu.VMEM((3, heads, rows, HEAD_DIM), F32),
                pltpu.VMEM((2, heads, HEAD_DIM, HEAD_DIM), F32),
                pltpu.VMEM((2, 5, heads, HEAD_DIM, HEAD_DIM), BF16),
                pltpu.VMEM((2, rows, rows), BF16),
                pltpu.VMEM((heads, 3, rows, HEAD_DIM), BF16),
                pltpu.VMEM((1, docs), jnp.int32),
                pltpu.SemaphoreType.DMA,
                pltpu.SemaphoreType.DMA((heads,)),
                pltpu.SemaphoreType.DMA((2, 3)),
                pltpu.SemaphoreType.DMA((2, 2, heads)),
                pltpu.SemaphoreType.DMA,
                pltpu.SemaphoreType.DMA,
                pltpu.SemaphoreType.DMA,
                pltpu.SemaphoreType.REGULAR,
            ],
            compiler_params=pltpu.CompilerParams(
                collective_id=0, has_side_effects=True
            ),
        )(queries, keys, values, out_grad, doc_lengths.reshape(1, -1))
        part = jax.ShapeDtypeStruct((rows_out, width * groups), BF16)
        return pl.pallas_call(
            split,
            out_shape=(part, part, part),
            in_specs=[pl.BlockSpec(memory_space=pltpu.VMEM)],
            out_specs=(pl.BlockSpec(memory_space=pl.ANY),) * 3,
            scratch_shapes=[pltpu.SemaphoreType.DMA((3,))],
            compiler_params=pltpu.CompilerParams(vmem_limit_bytes=8 << 20),
        )(out)

    return shards


def solution(mesh):
    return jax.shard_map(
        make_shards(mesh.shape["seq"], mesh.shape["head"]),
        mesh=mesh,
        in_specs=(P("seq", "head"), P("seq", "head"), P("seq", "head"), P("seq", "head"), P()),
        out_specs=(P(("seq", "head"), None), P(("seq", "head"), None), P(("seq", "head"), None)),
        check_vma=False,
    )
```

time: 27.8 us -> 26.2 us (0.942)
  Pallas kernels: 27 us -> 25.4 us
    pallas_call x1, Pallas kernels: 26 us -> 24.5 us  [shards(): pl.pallas_call(functools.partial(kernel, blocks, groups), out_shape=pltpu...]
where the time goes in v6:
time: 26.2 us; the launch traced here: 26 us
  Pallas kernels  25.4 us (97%)
  between operations  0.64 us (2%)
    pallas_call x1, Pallas kernels, shards(): pl.pallas_call(functools.partial(kernel, blocks, groups), out_shape=pltpu...  24.5 us
    pallas_call x1, Pallas kernels, shards(): pl.pallas_call(split, out_shape=(part, part, part), in_specs=[pl.BlockSpe...  0.9 us

profile of v6, /device:TPU:385, one launch (start us, length us, event | category | flops | bytes accessed | tf_op | source)
XLA Modules:
  0.0 26.0 jit_solution(9794087493139125880)
XLA Ops:
  0.6 24.5 %shard_map.76.whole_ref = bf16[3,32,4096]{2,1,0:T(8,128)(2,1)S(1)} custom-call(bf16[256,512]{1,0:T(8,128)(2,1)} %q_hbm.1, bf16[256,512]{1,0:T(8,128)(2,1)} %k_hbm.1, bf16[256,512]{1,0:T(8,128)(2,1)} %v_hbm.1, bf16[256,512]{1,0:T(8,128)(2,1)} %g_hbm.1, s32[1,32]{1,0:T(1,128)} %bitcast.1), custom_call_target="tpu_custom_call" | custom-call | tf_op jit(solution)/shard_map/pallas_call | solution.py:313
  25.1 0.9 %shard_map.77 = (bf16[32,4096]{1,0:T(8,128)(2,1)}, bf16[32,4096]{1,0:T(8,128)(2,1)}, bf16[32,4096]{1,0:T(8,128)(2,1)}) custom-call(bf16[3,32,4096]{2,1,0:T(8,128)(2,1)S(1)} %shard_map.76.whole_ref), custom_call_target="tpu_custom_call" | custom-call | tf_op jit(solution)/shard_map/pallas_call | solution.py:340

commit v7 on v6

--- a/solution.py
+++ b/solution.py
@@ -11,6 +11,7 @@
 MESH = pl.DeviceIdType.MESH
 F32 = jnp.float32
 BF16 = jnp.bfloat16
+
 
 NN = (((1,), (0,)), ((), ()))
 NT = (((1,), (1,)), ((), ()))
@@ -96,8 +97,6 @@
                 if s > 0:
                     pl.semaphore_signal(late_sem, inc=1, device_id={"seq": b + s}, device_id_type=MESH)
 
-    for load in sum(loads[1:], []):
-        load.start()
     table_load.wait()
 
     docs = len_ref.shape[1]
@@ -123,14 +122,6 @@
     first_rows = (lane_place < begin_next).astype(F32).astype(BF16)
     last_rows = (lane_place >= begin_last).astype(F32).astype(BF16)
 
-    same = lax.broadcasted_iota(jnp.int32, (rows, docs), 0).astype(F32) + begin_block
-    same = ((same >= starts) & (same < ends)).astype(F32).astype(BF16)
-    same = mm(same, same, NT)
-    row = lax.broadcasted_iota(jnp.int32, (rows, rows), 0)
-    col = lax.broadcasted_iota(jnp.int32, (rows, rows), 1)
-    pair[0] = jnp.where(col <= row, same, 0.0).astype(BF16)
-    pair[1] = jnp.where(col >= row, same, 0.0).astype(BF16)
-
     def to(way, kind):
         if kind == 0:
             return (b >= 2, b < blocks - 2)[1 - way]
@@ -196,7 +187,7 @@
     def pass_on(i):
         if i == 0:
             wait_late(after_late)
-        for way in (1, 0):
+        for way in (0, 1):
             @pl.when(came(way, 0))
             def _():
                 state_copy(i, way, 0).wait_recv()
@@ -257,14 +248,16 @@
     def finish(i):
         if i == 0:
             wait_late(beside_late)
+        arrive(i, 0)
+        query(i)
+        send_out(i, 0)
         arrive(i, 1)
         keys_values(i)
         send_out(i, 1)
-        arrive(i, 0)
-        query(i)
-        send_out(i, 0)
 
     loaded(0)
+    for load in sum(loads[1:], []):
+        load.start()
     states(0)
     enter()
     send_own(0)
@@ -272,7 +265,15 @@
         loaded(i)
         states(i)
         send_own(i)
-    half = max(heads // 2, 1)
+    same = lax.broadcasted_iota(jnp.int32, (rows, docs), 0).astype(F32) + begin_block
+    same = ((same >= starts) & (same < ends)).astype(F32).astype(BF16)
+    same = mm(same, same, NT)
+    row = lax.broadcasted_iota(jnp.int32, (rows, rows), 0)
+    col = lax.broadcasted_iota(jnp.int32, (rows, rows), 1)
+    pair[0] = jnp.where(col <= row, same, 0.0).astype(BF16)
+    pair[1] = jnp.where(col >= row, same, 0.0).astype(BF16)
+
+    half = 1
     for i in range(half):
         inner(i)
     for i in range(heads):
@@ -294,14 +295,12 @@
 
 
 def split(whole_ref, a_ref, b_ref, c_ref, sem):
-    copies = [
-        pltpu.make_async_copy(whole_ref.at[i], part, sem.at[i])
-        for i, part in enumerate((a_ref, b_ref, c_ref))
-    ]
-    for copy in copies:
-        copy.start()
-    for copy in copies:
-        copy.wait()
+    half = a_ref.shape[0] // 2
+    for i, part in enumerate((a_ref, b_ref, c_ref)):
+        for j in range(2):
+            some = pl.ds(j * half, half)
+            pltpu.make_async_copy(whole_ref.at[i, some], part.at[some], sem).start()
+    pltpu.make_async_copy(whole_ref, whole_ref, sem).wait()
 
 
 def make_shards(blocks, groups):
@@ -342,7 +341,7 @@
             out_shape=(part, part, part),
             in_specs=[pl.BlockSpec(memory_space=pltpu.VMEM)],
             out_specs=(pl.BlockSpec(memory_space=pl.ANY),) * 3,
-            scratch_shapes=[pltpu.SemaphoreType.DMA((3,))],
+            scratch_shapes=[pltpu.SemaphoreType.DMA],
             compiler_params=pltpu.CompilerParams(vmem_limit_bytes=8 << 20),
         )(out)
 

time: 26.2 us -> 25.9 us (0.989)
  Pallas kernels: 25.4 us -> 25.1 us
    pallas_call x1, Pallas kernels: 24.5 us -> 24.2 us  [shards(): pl.pallas_call(functools.partial(kernel, blocks, groups), out_shape=pltpu...]
where the time goes in v7:
time: 25.9 us; the launch traced here: 25.7 us
  Pallas kernels  25.1 us (97%)
  between operations  0.64 us (2%)
    pallas_call x1, Pallas kernels, shards(): pl.pallas_call(functools.partial(kernel, blocks, groups), out_shape=pltpu...  24.2 us
    pallas_call x1, Pallas kernels, shards(): pl.pallas_call(split, out_shape=(part, part, part), in_specs=[pl.BlockSpe...  0.88 us

profile of v7, /device:TPU:385, one launch (start us, length us, event | category | flops | bytes accessed | tf_op | source)
XLA Modules:
  0.0 25.7 jit_solution(5170402380894193098)
XLA Ops:
  0.6 24.2 %shard_map.76.whole_ref = bf16[3,32,4096]{2,1,0:T(8,128)(2,1)S(1)} custom-call(bf16[256,512]{1,0:T(8,128)(2,1)} %q_hbm.1, bf16[256,512]{1,0:T(8,128)(2,1)} %k_hbm.1, bf16[256,512]{1,0:T(8,128)(2,1)} %v_hbm.1, bf16[256,512]{1,0:T(8,128)(2,1)} %g_hbm.1, s32[1,32]{1,0:T(1,128)} %bitcast.1), custom_call_target="tpu_custom_call" | custom-call | tf_op jit(solution)/shard_map/pallas_call | solution.py:312
  24.9 0.9 %shard_map.77 = (bf16[32,4096]{1,0:T(8,128)(2,1)}, bf16[32,4096]{1,0:T(8,128)(2,1)}, bf16[32,4096]{1,0:T(8,128)(2,1)}) custom-call(bf16[3,32,4096]{2,1,0:T(8,128)(2,1)S(1)} %shard_map.76.whole_ref), custom_call_target="tpu_custom_call" | custom-call | tf_op jit(solution)/shard_map/pallas_call | solution.py:339

commit v8 on v7

--- a/solution.py
+++ b/solution.py
@@ -248,12 +248,10 @@
     def finish(i):
         if i == 0:
             wait_late(beside_late)
-        arrive(i, 0)
-        query(i)
-        send_out(i, 0)
-        arrive(i, 1)
-        keys_values(i)
-        send_out(i, 1)
+        for part in (1, 0) if i == heads - 1 else (0, 1):
+            arrive(i, part)
+            (query, keys_values)[part](i)
+            send_out(i, part)
 
     loaded(0)
     for load in sum(loads[1:], []):

time: 25.9 us -> 26 us (level)
  no operation moved by 1% of the time
where the time goes in v8:
time: 26 us; the launch traced here: 25.8 us
  Pallas kernels  25.1 us (97%)
  between operations  0.64 us (2%)
    pallas_call x1, Pallas kernels, shards(): pl.pallas_call(functools.partial(kernel, blocks, groups), out_shape=pltpu...  24.2 us
    pallas_call x1, Pallas kernels, shards(): pl.pallas_call(split, out_shape=(part, part, part), in_specs=[pl.BlockSpe...  0.88 us

profile of v8, /device:TPU:385, one launch (start us, length us, event | category | flops | bytes accessed | tf_op | source)
XLA Modules:
  0.0 25.8 jit_solution(1841941510354390301)
XLA Ops:
  0.6 24.2 %shard_map.76.whole_ref = bf16[3,32,4096]{2,1,0:T(8,128)(2,1)S(1)} custom-call(bf16[256,512]{1,0:T(8,128)(2,1)} %q_hbm.1, bf16[256,512]{1,0:T(8,128)(2,1)} %k_hbm.1, bf16[256,512]{1,0:T(8,128)(2,1)} %v_hbm.1, bf16[256,512]{1,0:T(8,128)(2,1)} %g_hbm.1, s32[1,32]{1,0:T(1,128)} %bitcast.1), custom_call_target="tpu_custom_call" | custom-call | tf_op jit(solution)/shard_map/pallas_call | solution.py:310
  24.9 0.9 %shard_map.77 = (bf16[32,4096]{1,0:T(8,128)(2,1)}, bf16[32,4096]{1,0:T(8,128)(2,1)}, bf16[32,4096]{1,0:T(8,128)(2,1)}) custom-call(bf16[3,32,4096]{2,1,0:T(8,128)(2,1)S(1)} %shard_map.76.whole_ref), custom_call_target="tpu_custom_call" | custom-call | tf_op jit(solution)/shard_map/pallas_call | solution.py:337

commit v9 on v8

--- a/solution.py
+++ b/solution.py
@@ -234,7 +234,7 @@
     def keys_values(i):
         high, low = whole(1, i)
         v = v_ref[:, cols(i)] * last_rows
-        made[i, 1] = (local[1, i] + (mm(v, high, NT) + mm(v, low, NT))).astype(BF16)
+        made[i, 1] = (local[1, i] + mm(twice(v), jnp.concatenate([high, low], axis=1), NT)).astype(BF16)
         k = k_ref[:, cols(i)] * last_rows
         both = jnp.concatenate([high, low], axis=0)
         made[i, 2] = (local[2, i] + mm(twice(k), both, NN)).astype(BF16)

time: 26 us -> 26 us (level)
  no operation moved by 1% of the time
where the time goes in v9:
time: 26 us; the launch traced here: 25.8 us
  Pallas kernels  25.1 us (97%)
  between operations  0.64 us (2%)
    pallas_call x1, Pallas kernels, shards(): pl.pallas_call(functools.partial(kernel, blocks, groups), out_shape=pltpu...  24.2 us
    pallas_call x1, Pallas kernels, shards(): pl.pallas_call(split, out_shape=(part, part, part), in_specs=[pl.BlockSpe...  0.88 us

profile of v9, /device:TPU:385, one launch (start us, length us, event | category | flops | bytes accessed | tf_op | source)
XLA Modules:
  0.0 25.8 jit_solution(1757678114695054274)
XLA Ops:
  0.6 24.2 %shard_map.76.whole_ref = bf16[3,32,4096]{2,1,0:T(8,128)(2,1)S(1)} custom-call(bf16[256,512]{1,0:T(8,128)(2,1)} %q_hbm.1, bf16[256,512]{1,0:T(8,128)(2,1)} %k_hbm.1, bf16[256,512]{1,0:T(8,128)(2,1)} %v_hbm.1, bf16[256,512]{1,0:T(8,128)(2,1)} %g_hbm.1, s32[1,32]{1,0:T(1,128)} %bitcast.1), custom_call_target="tpu_custom_call" | custom-call | tf_op jit(solution)/shard_map/pallas_call | solution.py:310
  24.9 0.9 %shard_map.77 = (bf16[32,4096]{1,0:T(8,128)(2,1)}, bf16[32,4096]{1,0:T(8,128)(2,1)}, bf16[32,4096]{1,0:T(8,128)(2,1)}) custom-call(bf16[3,32,4096]{2,1,0:T(8,128)(2,1)S(1)} %shard_map.76.whole_ref), custom_call_target="tpu_custom_call" | custom-call | tf_op jit(solution)/shard_map/pallas_call | solution.py:337
